TPU v7x, 32 devices: a whole 2x2x4 slice. The times are simulated.
32 devices in a mesh: fsdp: 2 (over x), context: 4 (over z), tensor: 4 (over y, core).
Axes of the slice: x: 2, y: 2, z: 4, core: 2. Of those that a mesh axis runs over, the one named last changes fastest.
Arguments:
- tokens: bfloat16 [4096, 960], P(('fsdp', 'context', 'tensor')), may hold values from -6 to 6
- positions: int32 [2, 2048], P('fsdp'), may hold values from 0 to 2047, as said below
- cotangent: bfloat16 [4096, 960], P(('fsdp', 'context', 'tensor')), may hold values from -6 to 6
- attn_gain: bfloat16 [960], P('fsdp'), may hold values from 0.099609375 to 1.8984375
- query_weight: bfloat16 [960, 960], P('fsdp'), as said below
- key_weight: bfloat16 [960, 320], P('fsdp'), as said below
- value_weight: bfloat16 [960, 320], P('fsdp'), may hold values from -0.1875 to 0.1875
- out_weight: bfloat16 [960, 960], P('fsdp'), may hold values from -1 to 1
- mlp_gain: bfloat16 [960], P('fsdp'), may hold values from 0.099609375 to 1.8984375
- gate_weight: bfloat16 [960, 2560], P('fsdp', 'tensor'), may hold values from -0.1875 to 0.1875
- up_weight: bfloat16 [960, 2560], P('fsdp', 'tensor'), may hold values from -0.1875 to 0.1875
- down_weight: bfloat16 [960, 2560], P('fsdp', 'tensor'), may hold values from -0.125 to 0.125
Outputs:
- output: bfloat16 [4096, 960], P(('fsdp', 'context', 'tensor'))
- input_grad: float32 [4096, 960], P(('fsdp', 'context', 'tensor'))
- attn_gain_grad: float32 [960], P('fsdp')
- query_grad: float32 [960, 960], P('fsdp')
- key_grad: float32 [960, 320], P('fsdp')
- value_grad: float32 [960, 320], P('fsdp')
- out_grad: float32 [960, 960], P('fsdp')
- mlp_gain_grad: float32 [960], P('fsdp')
- gate_grad: float32 [960, 2560], P('fsdp', 'tensor')
- up_grad: float32 [960, 2560], P('fsdp', 'tensor')
- down_grad: float32 [960, 2560], P('fsdp', 'tensor')
Inputs may be any that keep to these rules, and one draw needn't show every extreme that they name: Each sequence holds every position from 0 once; its rows form blocks of 64 rows of consecutive rising positions, each block starting at a multiple of 64. `query_weight`: entries of either sign. `key_weight`: entries of either sign.
All inputs are finite; a program needn't handle non-finite values.
Results may differ from a plain program's by a relative error of at most 0.025.
The roundings to bfloat16 on the way count: a program that leaves them out, or rounds other values in their place, can miss the bound.
Values may be sent and summed in bfloat16 or wider, within the bound.
A program may use at most 128 MiB of HBM per device.

v0:
```python
import jax
import jax.numpy as jnp
from jax import lax
from jax.sharding import PartitionSpec as P

HEADS = 15
KV_HEADS = 5
HD = 64


EPS = 1e-05
THETA = 100000.0
NEG = -1e30
ROWS_MATCH = (((0,), (0,)), ((), ()))
COLS_MATCH = (((1,), (1,)), ((), ()))


def norm_scale(values):
    return lax.rsqrt(jnp.mean(values * values, axis=1, keepdims=True) + EPS)


def norm_back(grad, hat, scale, gain):
    weighted = grad * gain
    return scale * (weighted - hat * jnp.mean(weighted * hat, axis=1, keepdims=True))


def rotary_tables(places):
    half = HD // 2
    freq = THETA ** (-2.0 * jnp.arange(half, dtype=jnp.float32) / HD)
    angle = places.astype(jnp.float32)[:, None] * freq[None, :]
    cosine = jnp.concatenate([jnp.cos(angle), jnp.cos(angle)], axis=1)[:, None, :]
    sine = jnp.concatenate([jnp.sin(angle), jnp.sin(angle)], axis=1)[:, None, :]
    return (cosine, sine)


def rotate(values, cosine, sine):
    half = values.shape[-1] // 2
    turned = jnp.concatenate([-values[..., half:], values[..., :half]], axis=-1)
    return values * cosine + turned * sine


def unrotate(values, cosine, sine):
    half = values.shape[-1] // 2
    scaled = values * sine
    return values * cosine + jnp.concatenate([scaled[..., half:], -scaled[..., :half]], axis=-1)


def key_blocks(all_keys, all_values, sequence_places):
    total = all_keys.shape[0]
    block = min(512, total)
    count = total // block
    keys = all_keys.reshape(count, block, KV_HEADS, HD)
    values = all_values.reshape(count, block, KV_HEADS, HD)
    return (keys, values, sequence_places.reshape(count, block))


def block_scores(q_rot, own_places, key_block, place_block):
    scores = jnp.einsum(
        "qgrd,kgd->grqk", q_rot, key_block, preferred_element_type=jnp.float32
    ) * HD ** (-0.5)
    mask = place_block[None, :] <= own_places[:, None]
    return (jnp.where(mask, scores, NEG), mask)


def attend_forward(q_rot, own_places, all_keys, all_values, sequence_places):
    rows = q_rot.shape[0]
    groups = q_rot.shape[2]
    blocks = key_blocks(all_keys, all_values, sequence_places)

    def measure(carry, piece):
        peak, summed = carry
        key_block, value_block, place_block = piece
        scores, mask = block_scores(q_rot, own_places, key_block, place_block)
        new_peak = jnp.maximum(peak, jnp.max(scores, axis=-1))
        shrink = jnp.exp(peak - new_peak)
        weights = jnp.where(mask, jnp.exp(scores - new_peak[..., None]), 0.0)
        summed = summed * shrink + jnp.sum(weights, axis=-1)
        return ((new_peak, summed), None)

    start_peak = jnp.full((KV_HEADS, groups, rows), NEG, jnp.float32)
    start_sum = jnp.zeros((KV_HEADS, groups, rows), jnp.float32)
    (peak, summed), _ = lax.scan(measure, (start_peak, start_sum), blocks)
    totals = peak + jnp.log(summed)

    def combine(accum, piece):
        key_block, value_block, place_block = piece
        scores, mask = block_scores(q_rot, own_places, key_block, place_block)
        probs = jnp.where(mask, jnp.exp(scores - totals[..., None]), 0.0).astype(jnp.bfloat16)
        accum = accum + jnp.einsum(
            "grqk,kgd->grqd", probs, value_block, preferred_element_type=jnp.float32
        )
        return (accum, None)

    start_accum = jnp.zeros((KV_HEADS, groups, rows, HD), jnp.float32)
    accum, _ = lax.scan(combine, start_accum, blocks)
    attended = (
        jnp.transpose(accum, (2, 0, 1, 3))
        .reshape(rows, KV_HEADS * groups * HD)
        .astype(jnp.bfloat16)
    )
    return (attended, totals)


def attend_backward(
    q_rot, own_places, all_keys, all_values, sequence_places, totals, d_att4, delta
):
    rows = q_rot.shape[0]
    groups = q_rot.shape[2]
    blocks = key_blocks(all_keys, all_values, sequence_places)

    def step(d_query, piece):
        key_block, value_block, place_block = piece
        scores, mask = block_scores(q_rot, own_places, key_block, place_block)
        probs = jnp.where(mask, jnp.exp(scores - totals[..., None]), 0.0)
        d_probs = jnp.einsum(
            "qgrd,kgd->grqk", d_att4, value_block, preferred_element_type=jnp.float32
        )
        d_scores = (probs * (d_probs - delta[..., None]) * HD ** (-0.5)).astype(jnp.bfloat16)
        d_query = d_query + jnp.einsum(
            "grqk,kgd->qgrd", d_scores, key_block, preferred_element_type=jnp.float32
        )
        d_key = jnp.einsum("grqk,qgrd->kgd", d_scores, q_rot, preferred_element_type=jnp.float32)
        d_value = jnp.einsum(
            "grqk,qgrd->kgd", probs.astype(jnp.bfloat16), d_att4, preferred_element_type=jnp.float32
        )
        return (d_query, (d_key, d_value))

    start = jnp.zeros((rows, KV_HEADS, groups, HD), jnp.float32)
    d_query, (d_keys, d_values) = lax.scan(step, start, blocks)
    total = all_keys.shape[0]
    return (d_query, d_keys.reshape(total, KV_HEADS * HD), d_values.reshape(total, KV_HEADS * HD))


def per_device(
    tokens,
    positions,
    cotangent,
    attn_gain,
    query_weight,
    key_weight,
    value_weight,
    out_weight,
    mlp_gain,
    gate_weight,
    up_weight,
    down_weight,
):
    rows = tokens.shape[0]
    groups = HEADS // KV_HEADS
    place = lax.axis_index(("context", "tensor"))
    sequence_places = positions[0]
    own_places = lax.dynamic_slice_in_dim(sequence_places, place * rows, rows, 0)
    (
        gain_one,
        gain_two,
        query_full,
        key_full,
        value_full,
        out_full,
        gate_full,
        up_full,
        down_full,
    ) = (
        lax.all_gather(attn_gain, "fsdp", axis=0, tiled=True),
        lax.all_gather(mlp_gain, "fsdp", axis=0, tiled=True),
        lax.all_gather(query_weight, "fsdp", axis=0, tiled=True),
        lax.all_gather(key_weight, "fsdp", axis=0, tiled=True),
        lax.all_gather(value_weight, "fsdp", axis=0, tiled=True),
        lax.all_gather(out_weight, "fsdp", axis=0, tiled=True),
        lax.all_gather(gate_weight, "fsdp", axis=0, tiled=True),
        lax.all_gather(up_weight, "fsdp", axis=0, tiled=True),
        lax.all_gather(down_weight, "fsdp", axis=0, tiled=True),
    )
    inputs = tokens.astype(jnp.float32)
    first_scale = norm_scale(inputs)
    normed_one = (inputs * first_scale * gain_one.astype(jnp.float32)).astype(jnp.bfloat16)
    cosine, sine = rotary_tables(own_places)
    query = jnp.dot(normed_one, query_full, preferred_element_type=jnp.float32).reshape(
        rows, HEADS, HD
    )
    key_raw = jnp.dot(normed_one, key_full, preferred_element_type=jnp.float32).reshape(
        rows, KV_HEADS, HD
    )
    value = jnp.dot(normed_one, value_full, preferred_element_type=jnp.float32).astype(jnp.bfloat16)
    q_rot = rotate(query, cosine, sine).astype(jnp.bfloat16).reshape(rows, KV_HEADS, groups, HD)
    k_rot = rotate(key_raw, cosine, sine).astype(jnp.bfloat16).reshape(rows, KV_HEADS * HD)
    all_keys, all_values = (
        lax.all_gather(k_rot, ("context", "tensor"), axis=0, tiled=True),
        lax.all_gather(value, ("context", "tensor"), axis=0, tiled=True),
    )
    attended, totals = attend_forward(q_rot, own_places, all_keys, all_values, sequence_places)
    residual = inputs + jnp.dot(attended, out_full, preferred_element_type=jnp.float32)
    second_scale = norm_scale(residual)
    normed_two = (residual * second_scale * gain_two.astype(jnp.float32)).astype(jnp.bfloat16)
    mlp_rows = lax.all_gather(normed_two, "tensor", axis=0, tiled=True)
    gate = jnp.dot(mlp_rows, gate_full, preferred_element_type=jnp.float32)
    up = jnp.dot(mlp_rows, up_full, preferred_element_type=jnp.float32)
    act = (jax.nn.silu(gate) * up).astype(jnp.bfloat16)
    feed = lax.psum_scatter(
        lax.dot_general(act, down_full, COLS_MATCH, preferred_element_type=jnp.float32),
        "tensor",
        scatter_dimension=0,
        tiled=True,
    )
    output = (residual + feed).astype(jnp.bfloat16)
    (
        gain_one,
        gain_two,
        query_full,
        key_full,
        value_full,
        out_full,
        gate_full,
        up_full,
        down_full,
    ) = (
        lax.all_gather(attn_gain, "fsdp", axis=0, tiled=True),
        lax.all_gather(mlp_gain, "fsdp", axis=0, tiled=True),
        lax.all_gather(query_weight, "fsdp", axis=0, tiled=True),
        lax.all_gather(key_weight, "fsdp", axis=0, tiled=True),
        lax.all_gather(value_weight, "fsdp", axis=0, tiled=True),
        lax.all_gather(out_weight, "fsdp", axis=0, tiled=True),
        lax.all_gather(gate_weight, "fsdp", axis=0, tiled=True),
        lax.all_gather(up_weight, "fsdp", axis=0, tiled=True),
        lax.all_gather(down_weight, "fsdp", axis=0, tiled=True),
    )
    cot_rows = lax.all_gather(cotangent, "tensor", axis=0, tiled=True)
    d_act = jnp.dot(cot_rows, down_full, preferred_element_type=jnp.float32)
    down_grad = lax.dot_general(cot_rows, act, ROWS_MATCH, preferred_element_type=jnp.float32)
    sig = jax.nn.sigmoid(gate)
    d_gate = (d_act * up * sig * (1.0 + gate * (1.0 - sig))).astype(jnp.bfloat16)
    d_up = (d_act * gate * sig).astype(jnp.bfloat16)
    gate_grad = lax.dot_general(mlp_rows, d_gate, ROWS_MATCH, preferred_element_type=jnp.float32)
    up_grad = lax.dot_general(mlp_rows, d_up, ROWS_MATCH, preferred_element_type=jnp.float32)
    first = lax.dot_general(d_gate, gate_full, COLS_MATCH, preferred_element_type=jnp.float32)
    d_normed_two = lax.psum_scatter(
        first + lax.dot_general(d_up, up_full, COLS_MATCH, preferred_element_type=jnp.float32),
        "tensor",
        scatter_dimension=0,
        tiled=True,
    )
    hat_two = residual * second_scale
    mlp_gain_grad = jnp.sum(d_normed_two * hat_two, axis=0)
    d_residual = cotangent.astype(jnp.float32) + norm_back(
        d_normed_two, hat_two, second_scale, gain_two.astype(jnp.float32)
    )
    residual_round = d_residual.astype(jnp.bfloat16)
    d_attended = lax.dot_general(
        residual_round, out_full, COLS_MATCH, preferred_element_type=jnp.float32
    ).astype(jnp.bfloat16)
    delta = jnp.sum(
        (d_attended.astype(jnp.float32) * attended.astype(jnp.float32)).reshape(
            rows, KV_HEADS, groups, HD
        ),
        axis=-1,
    )
    delta = jnp.transpose(delta, (1, 2, 0))
    d_att4 = d_attended.reshape(rows, KV_HEADS, groups, HD)
    d_query, key_terms, value_terms = attend_backward(
        q_rot, own_places, all_keys, all_values, sequence_places, totals, d_att4, delta
    )
    own_dkey, own_dvalue = (
        lax.psum_scatter(key_terms, ("context", "tensor"), scatter_dimension=0, tiled=True),
        lax.psum_scatter(value_terms, ("context", "tensor"), scatter_dimension=0, tiled=True),
    )
    dq_rot = (
        unrotate(d_query.reshape(rows, HEADS, HD), cosine, sine)
        .astype(jnp.bfloat16)
        .reshape(rows, HEADS * HD)
    )
    dk_rot = (
        unrotate(own_dkey.reshape(rows, KV_HEADS, HD), cosine, sine)
        .astype(jnp.bfloat16)
        .reshape(rows, KV_HEADS * HD)
    )
    dv_round = own_dvalue.astype(jnp.bfloat16)
    d_normed_one = lax.dot_general(
        dq_rot, query_full, COLS_MATCH, preferred_element_type=jnp.float32
    )
    d_normed_one = d_normed_one + lax.dot_general(
        dk_rot, key_full, COLS_MATCH, preferred_element_type=jnp.float32
    )
    d_normed_one = d_normed_one + lax.dot_general(
        dv_round, value_full, COLS_MATCH, preferred_element_type=jnp.float32
    )
    hat_one = inputs * first_scale
    attn_gain_grad = jnp.sum(d_normed_one * hat_one, axis=0)
    input_grad = d_residual + norm_back(
        d_normed_one, hat_one, first_scale, gain_one.astype(jnp.float32)
    )
    normed_rows, attended_rows = (
        lax.all_gather(normed_one, "tensor", axis=0, tiled=True),
        lax.all_gather(attended, "tensor", axis=0, tiled=True),
    )
    query_cols, key_cols, value_cols, residual_cols = (
        lax.all_to_all(dq_rot, "tensor", split_axis=1, concat_axis=0, tiled=True),
        lax.all_to_all(dk_rot, "tensor", split_axis=1, concat_axis=0, tiled=True),
        lax.all_to_all(dv_round, "tensor", split_axis=1, concat_axis=0, tiled=True),
        lax.all_to_all(residual_round, "tensor", split_axis=1, concat_axis=0, tiled=True),
    )
    query_grad = lax.dot_general(
        normed_rows, query_cols, ROWS_MATCH, preferred_element_type=jnp.float32
    )
    key_grad = lax.dot_general(
        normed_rows, key_cols, ROWS_MATCH, preferred_element_type=jnp.float32
    )
    value_grad = lax.dot_general(
        normed_rows, value_cols, ROWS_MATCH, preferred_element_type=jnp.float32
    )
    out_grad = lax.dot_general(
        attended_rows, residual_cols, ROWS_MATCH, preferred_element_type=jnp.float32
    )
    attn_gain_grad, mlp_gain_grad = lax.psum((attn_gain_grad, mlp_gain_grad), "tensor")
    shares = (
        lax.psum_scatter(attn_gain_grad, ("fsdp", "context"), scatter_dimension=0, tiled=True),
        lax.psum_scatter(query_grad, ("fsdp", "context"), scatter_dimension=0, tiled=True),
        lax.psum_scatter(key_grad, ("fsdp", "context"), scatter_dimension=0, tiled=True),
        lax.psum_scatter(value_grad, ("fsdp", "context"), scatter_dimension=0, tiled=True),
        lax.psum_scatter(out_grad, ("fsdp", "context"), scatter_dimension=0, tiled=True),
        lax.psum_scatter(mlp_gain_grad, ("fsdp", "context"), scatter_dimension=0, tiled=True),
        lax.psum_scatter(gate_grad, ("fsdp", "context"), scatter_dimension=0, tiled=True),
        lax.psum_scatter(up_grad, ("fsdp", "context"), scatter_dimension=0, tiled=True),
        lax.psum_scatter(down_grad, ("fsdp", "context"), scatter_dimension=0, tiled=True),
    )
    merged = tuple(shares)
    owned = (
        lax.all_gather(merged[0], "context", axis=0, tiled=True),
        lax.all_gather(merged[1], "context", axis=0, tiled=True),
        lax.all_gather(merged[2], "context", axis=0, tiled=True),
        lax.all_gather(merged[3], "context", axis=0, tiled=True),
        lax.all_gather(merged[4], "context", axis=0, tiled=True),
        lax.all_gather(merged[5], "context", axis=0, tiled=True),
        lax.all_gather(merged[6], "context", axis=0, tiled=True),
        lax.all_gather(merged[7], "context", axis=0, tiled=True),
        lax.all_gather(merged[8], "context", axis=0, tiled=True),
    )
    owned = tuple(owned)
    whole_query, whole_key, whole_value, whole_out = (
        lax.all_gather(owned[1], "tensor", axis=1, tiled=True),
        lax.all_gather(owned[2], "tensor", axis=1, tiled=True),
        lax.all_gather(owned[3], "tensor", axis=1, tiled=True),
        lax.all_gather(owned[4], "tensor", axis=1, tiled=True),
    )
    owned = (
        owned[0],
        whole_query,
        whole_key,
        whole_value,
        whole_out,
        owned[5],
        owned[6],
        owned[7],
        owned[8],
    )
    return (
        output,
        input_grad,
        owned[0],
        owned[1],
        owned[2],
        owned[3],
        owned[4],
        owned[5],
        owned[6],
        owned[7],
        owned[8],
    )


def solution(mesh):
    return jax.shard_map(
        per_device,
        mesh=mesh,
        in_specs=(
            P(("fsdp", "context", "tensor"), None),
            P("fsdp", None),
            P(("fsdp", "context", "tensor"), None),
            P("fsdp"),
            P("fsdp", None),
            P("fsdp", None),
            P("fsdp", None),
            P("fsdp", None),
            P("fsdp"),
            P("fsdp", "tensor"),
            P("fsdp", "tensor"),
            P("fsdp", "tensor"),
        ),
        out_specs=(
            P(("fsdp", "context", "tensor"), None),
            P(("fsdp", "context", "tensor"), None),
            P("fsdp"),
            P("fsdp", None),
            P("fsdp", None),
            P("fsdp", None),
            P("fsdp", None),
            P("fsdp"),
            P("fsdp", "tensor"),
            P("fsdp", "tensor"),
            P("fsdp", "tensor"),
        ),
        check_vma=False,
    )
```

profile of v0, /device:TPU:0, one launch (start us, length us, event | category | flops | bytes accessed | tf_op | source)
XLA Modules:
  0.0 1048.0 jit_solution(14009848961512914595)
XLA Ops:
  11.7 5.8 all-reduce.15
  17.5 16.5 %all-gather = bf16[2,480,320]{1,2,0:T(8,128)(2,1)S(1)} all-gather(bf16[1,480,320]{1,2,0:T(8,128)(2,1)} %bitcast.331), channel_id=1, replica_groups=mesh['fsdp'=2,'context'=4,'tensor'=4] {'fsdp'}, dimensions={0}, use_global_device_ids=true | all-gather | bytes 921600 | tf_op jit(solution)/shard_map/all_gather | solution.py:167
  37.1 17.0 %all-gather.1 = bf16[2,480,320]{1,2,0:T(8,128)(2,1)S(1)} all-gather(bf16[1,480,320]{1,2,0:T(8,128)(2,1)S(1)} %bitcast.332), channel_id=1, replica_groups=mesh['fsdp'=2,'context'=4,'tensor'=4] {'fsdp'}, dimensions={0}, use_global_device_ids=true | all-gather | bytes 921600 | tf_op jit(solution)/shard_map/all_gather | solution.py:168
  60.2 9.9 all_gather.105
  72.7 24.5 %all-gather.17.cloned.1.call-done = bf16[2048,320]{0,1:T(8,128)(2,1)} async-done(((bf16[128,320]{0,1:T(8,128)(2,1)}), bf16[2048,320]{0,1:T(8,128)(2,1)}) %all-gather.17.cloned.1.call-update) | async-done | bytes 1310736 | tf_op jit(solution)/shard_map/all_gather | solution.py:188
  97.3 4.1 reshape.140
  104.0 27.9 %while.39 = (s32[]{:T(128)}, f32[5,3,128]{2,1,0:T(4,128)S(1)}, f32[5,3,128]{2,1,0:T(4,128)S(1)}, s32[4,512]{1,0:T(4,128)S(1)}, s32[128]{0:T(128)S(1)}, /*index=5...) while((s32[]{:T(128)}, f32[5,3,128]{2,1,0:T(4,128)S(1)}, ...), condition=%wide.region_4.5_spmd.clone, body=%wide.region_1.4_spmd.clone.sunk | while | flops 133768576 | bytes 8740984 | solution.py:82
  131.9 5.0 all-gather.21.cloned.1.call-done
  136.9 4.1 reshape.143
  143.6 11.0 %while.40 = (s32[]{:T(128)}, f32[5,3,128,64]{2,3,1,0:T(8,128)S(1)}, s32[4,512]{1,0:T(4,128)S(1)}, s32[128]{0:T(128)S(1)}, bf16[4,512,5,64]{1,3,2,0:T(8,128)(2,1)...) while((s32[]{:T(128)}, f32[5,3,128,64]{2,3,1,0:T(8,128)S(1)}, ...), condition=%wide.region_6.7_spmd.clone, body=%wide.region_5.6_spmd.clone.sunk | while | flops 256884736 | bytes 2031226 | solution.py:95
  154.7 14.6 %all-gather.23.cloned.1.call-done = bf16[960,960]{1,0:T(8,128)(2,1)} async-done(((bf16[480,960]{1,0:T(8,128)(2,1)}), bf16[960,960]{1,0:T(8,128)(2,1)}) %all-gather.23.cloned.1.call-update) | async-done | bytes 1843216 | tf_op jit(solution)/shard_map/all_gather | solution.py:169
  171.9 9.8 all_gather.101
  181.7 12.2 %all-gather.25.cloned.1.call-done = bf16[960,640]{1,0:T(8,128)(2,1)} async-done(((bf16[480,640]{1,0:T(8,128)(2,1)}), bf16[960,640]{1,0:T(8,128)(2,1)}) %all-gather.25.cloned.1.call-update) | async-done | bytes 1228816 | tf_op jit(solution)/shard_map/all_gather | solution.py:170
  197.3 21.4 %all-gather.27.cloned.1.call-done = bf16[960,640]{1,0:T(8,128)(2,1)} async-done(((bf16[480,640]{1,0:T(8,128)(2,1)}), bf16[960,640]{1,0:T(8,128)(2,1)}) %all-gather.27.cloned.1.call-update) | async-done | bytes 1228816 | tf_op jit(solution)/shard_map/all_gather | solution.py:171
  222.1 21.5 %all-gather.29.cloned.1.call-done = bf16[960,640]{1,0:T(8,128)(2,1)} async-done(((bf16[480,640]{1,0:T(8,128)(2,1)}), bf16[960,640]{1,0:T(8,128)(2,1)}) %all-gather.29.cloned.1.call-update) | async-done | bytes 1228816 | tf_op jit(solution)/shard_map/all_gather | solution.py:172
  243.6 4.4 multiply_convert_fusion
  263.0 19.5 %reduce-scatter.20.cloned.1.call-done = f32[128,960]{0,1:T(8,128)} async-done(((f32[512,960]{0,1:T(8,128)}), f32[128,960]{0,1:T(8,128)}) %reduce-scatter.20.cloned.1.call-update) | async-done | bytes 491536 | tf_op jit(solution)/shard_map/reduce_scatter | solution.py:236
  290.7 155.8 %while.41 = (s32[]{:T(128)}, f32[128,5,3,64]{0,3,2,1:T(8,128)S(1)}, f32[4,512,5,64]{1,0,3,2:T(4,128)}, f32[4,512,5,64]{1,0,3,2:T(4,128)}, bf16[4,512,5,64]{1,3,2...) while((s32[]{:T(128)}, f32[128,5,3,64]{0,3,2,1:T(8,128)S(1)}, ...), condition=%wide.region_13.14_spmd.clone, body=%wide.region_12.13_spmd.clone.sunk | while | flops 642236416 | bytes 45213528 | solution.py:129
  298.5 13.6 %dynamic_update_slice.11 = f32[4,512,5,64]{1,0,3,2:T(4,128)} dynamic-update-slice(f32[4,512,5,64]{1,0,3,2:T(4,128)} %get-tuple-element.704, f32[1,512,5,64]{1,0,3,2:T(1,128)S(1)} %copy.144, s32[]{:T(128)S(6)} %copy.169, s32[]{:T(128)} %constant.78.clone.1..sunk.2, s32[]{:T(128)} %constant.78.clone.1..sunk.2, s32[]{:T(128)} %constant.78.clone.1..sunk.2) | dynamic-update-slice | bytes 1310724 | tf_op jit(solution)/shard_map/while/body/jit(dynamic_update_index_in_dim)/dynamic_update_slice | solution.py:129
  316.1 13.6 %dynamic_update_slice.12 = f32[4,512,5,64]{1,0,3,2:T(4,128)} dynamic-update-slice(f32[4,512,5,64]{1,0,3,2:T(4,128)} %get-tuple-element.705, f32[1,512,5,64]{1,0,3,2:T(1,128)S(1)} %copy.145, s32[]{:T(128)S(6)} %copy.169, s32[]{:T(128)} %constant.78.clone.1..sunk.2, s32[]{:T(128)} %constant.78.clone.1..sunk.2, s32[]{:T(128)} %constant.78.clone.1..sunk.2) | dynamic-update-slice | bytes 1310724 | tf_op jit(solution)/shard_map/while/body/jit(dynamic_update_index_in_dim)/dynamic_update_slice | solution.py:129
  337.5 13.6 %dynamic_update_slice.11 = f32[4,512,5,64]{1,0,3,2:T(4,128)} dynamic-update-slice(f32[4,512,5,64]{1,0,3,2:T(4,128)} %get-tuple-element.704, f32[1,512,5,64]{1,0,3,2:T(1,128)S(1)} %copy.144, s32[]{:T(128)S(6)} %copy.169, s32[]{:T(128)} %constant.78.clone.1..sunk.2, s32[]{:T(128)} %constant.78.clone.1..sunk.2, s32[]{:T(128)} %constant.78.clone.1..sunk.2) | dynamic-update-slice | bytes 1310724 | tf_op jit(solution)/shard_map/while/body/jit(dynamic_update_index_in_dim)/dynamic_update_slice | solution.py:129
  355.0 13.6 %dynamic_update_slice.12 = f32[4,512,5,64]{1,0,3,2:T(4,128)} dynamic-update-slice(f32[4,512,5,64]{1,0,3,2:T(4,128)} %get-tuple-element.705, f32[1,512,5,64]{1,0,3,2:T(1,128)S(1)} %copy.145, s32[]{:T(128)S(6)} %copy.169, s32[]{:T(128)} %constant.78.clone.1..sunk.2, s32[]{:T(128)} %constant.78.clone.1..sunk.2, s32[]{:T(128)} %constant.78.clone.1..sunk.2) | dynamic-update-slice | bytes 1310724 | tf_op jit(solution)/shard_map/while/body/jit(dynamic_update_index_in_dim)/dynamic_update_slice | solution.py:129
  376.4 13.6 %dynamic_update_slice.11 = f32[4,512,5,64]{1,0,3,2:T(4,128)} dynamic-update-slice(f32[4,512,5,64]{1,0,3,2:T(4,128)} %get-tuple-element.704, f32[1,512,5,64]{1,0,3,2:T(1,128)S(1)} %copy.144, s32[]{:T(128)S(6)} %copy.169, s32[]{:T(128)} %constant.78.clone.1..sunk.2, s32[]{:T(128)} %constant.78.clone.1..sunk.2, s32[]{:T(128)} %constant.78.clone.1..sunk.2) | dynamic-update-slice | bytes 1310724 | tf_op jit(solution)/shard_map/while/body/jit(dynamic_update_index_in_dim)/dynamic_update_slice | solution.py:129
  394.0 13.6 %dynamic_update_slice.12 = f32[4,512,5,64]{1,0,3,2:T(4,128)} dynamic-update-slice(f32[4,512,5,64]{1,0,3,2:T(4,128)} %get-tuple-element.705, f32[1,512,5,64]{1,0,3,2:T(1,128)S(1)} %copy.145, s32[]{:T(128)S(6)} %copy.169, s32[]{:T(128)} %constant.78.clone.1..sunk.2, s32[]{:T(128)} %constant.78.clone.1..sunk.2, s32[]{:T(128)} %constant.78.clone.1..sunk.2) | dynamic-update-slice | bytes 1310724 | tf_op jit(solution)/shard_map/while/body/jit(dynamic_update_index_in_dim)/dynamic_update_slice | solution.py:129
  415.4 13.6 %dynamic_update_slice.11 = f32[4,512,5,64]{1,0,3,2:T(4,128)} dynamic-update-slice(f32[4,512,5,64]{1,0,3,2:T(4,128)} %get-tuple-element.704, f32[1,512,5,64]{1,0,3,2:T(1,128)S(1)} %copy.144, s32[]{:T(128)S(6)} %copy.169, s32[]{:T(128)} %constant.78.clone.1..sunk.2, s32[]{:T(128)} %constant.78.clone.1..sunk.2, s32[]{:T(128)} %constant.78.clone.1..sunk.2) | dynamic-update-slice | bytes 1310724 | tf_op jit(solution)/shard_map/while/body/jit(dynamic_update_index_in_dim)/dynamic_update_slice | solution.py:129
  432.9 13.6 %dynamic_update_slice.12 = f32[4,512,5,64]{1,0,3,2:T(4,128)} dynamic-update-slice(f32[4,512,5,64]{1,0,3,2:T(4,128)} %get-tuple-element.705, f32[1,512,5,64]{1,0,3,2:T(1,128)S(1)} %copy.145, s32[]{:T(128)S(6)} %copy.169, s32[]{:T(128)} %constant.78.clone.1..sunk.2, s32[]{:T(128)} %constant.78.clone.1..sunk.2, s32[]{:T(128)} %constant.78.clone.1..sunk.2) | dynamic-update-slice | bytes 1310724 | tf_op jit(solution)/shard_map/while/body/jit(dynamic_update_index_in_dim)/dynamic_update_slice | solution.py:129
  446.5 4.4 copy.124
  451.0 4.4 copy.125
  460.6 11.9 %all_gather.107 = bf16[512,960]{0,1:T(8,128)(2,1)S(1)} all-gather(bf16[128,960]{0,1:T(8,128)(2,1)S(1)} %fusion.55), channel_id=1, replica_groups=mesh['fsdp'=2,'context'=4,'tensor'=4] {'tensor'}, dimensions={0}, use_global_device_ids=true | all-gather | bytes 1228800 | tf_op jit(solution)/shard_map/all_gather | solution.py:292
  477.4 11.9 %all_gather.114 = bf16[512,960]{0,1:T(8,128)(2,1)S(1)} all-gather(bf16[128,960]{0,1:T(8,128)(2,1)S(1)} %bitcast.322), channel_id=1, replica_groups=mesh['fsdp'=2,'context'=4,'tensor'=4] {'tensor'}, dimensions={0}, use_global_device_ids=true | all-gather | bytes 1228800 | tf_op jit(solution)/shard_map/all_gather | solution.py:293
  491.9 11.3 %reduce-scatter.34.cloned.1.call-done = f32[120,640]{1,0:T(8,128)} async-done(((f32[960,640]{1,0:T(8,128)}), f32[120,640]{1,0:T(8,128)}) %reduce-scatter.34.cloned.1.call-update) | async-done | bytes 307216
  507.2 62.6 %reduce-scatter.22.cloned.1.call-done = f32[128,320]{0,1:T(8,128)} async-done(((f32[2048,320]{0,1:T(8,128)}), f32[128,320]{0,1:T(8,128)}) %reduce-scatter.22.cloned.1.call-update) | async-done | bytes 163856 | tf_op jit(solution)/shard_map/reduce_scatter | solution.py:263
  575.7 61.2 %reduce-scatter.24.cloned.1.call-done = f32[128,320]{0,1:T(8,128)} async-done(((f32[2048,320]{0,1:T(8,128)}), f32[128,320]{0,1:T(8,128)}) %reduce-scatter.24.cloned.1.call-update) | async-done | bytes 163856 | tf_op jit(solution)/shard_map/reduce_scatter | solution.py:264
  647.2 56.6 %reduce-scatter.26.cloned.1.call-done = f32[120,240]{1,0:T(8,128)} async-done(((f32[960,240]{1,0:T(8,128)}), f32[120,240]{1,0:T(8,128)}) %reduce-scatter.26.cloned.1.call-update) | async-done | bytes 115216 | tf_op jit(solution)/shard_map/reduce_scatter | solution.py:316
  703.8 16.3 %all_gather.108 = f32[480,240]{1,0:T(8,128)S(1)} all-gather(f32[120,240]{1,0:T(8,128)} %reduce-scatter.26.cloned.1.call-done), channel_id=1, replica_groups=mesh['fsdp'=2,'context'=4,'tensor'=4] {'context'}, dimensions={0}, use_global_device_ids=true | all-gather | bytes 576000 | tf_op jit(solution)/shard_map/all_gather | solution.py:328
  721.1 49.6 %reduce-scatter.28.cloned.1.call-done = f32[120,240]{1,0:T(8,128)} async-done(((f32[960,240]{1,0:T(8,128)}), f32[120,240]{1,0:T(8,128)}) %reduce-scatter.28.cloned.1.call-update) | async-done | bytes 115216 | tf_op jit(solution)/shard_map/reduce_scatter | solution.py:319
  770.7 17.9 %all_gather.115 = f32[480,240]{1,0:T(8,128)S(1)} all-gather(f32[120,240]{1,0:T(8,128)} %reduce-scatter.28.cloned.1.call-done), channel_id=1, replica_groups=mesh['fsdp'=2,'context'=4,'tensor'=4] {'context'}, dimensions={0}, use_global_device_ids=true | all-gather | bytes 576000 | tf_op jit(solution)/shard_map/all_gather | solution.py:331
  794.0 10.2 all-gather.35.cloned.1.call-done
  804.1 31.4 %all-gather.37.cloned.1.call-done = f32[480,640]{1,0:T(8,128)} async-done(((f32[120,640]{1,0:T(8,128)}), f32[480,640]{1,0:T(8,128)}) %all-gather.37.cloned.1.call-update) | async-done | bytes 1228816 | tf_op jit(solution)/shard_map/all_gather | solution.py:334
  835.6 31.7 %all-gather.39.cloned.1.call-done = f32[480,640]{1,0:T(8,128)} async-done(((f32[120,640]{1,0:T(8,128)}), f32[480,640]{1,0:T(8,128)}) %all-gather.39.cloned.1.call-update) | async-done | bytes 1228816 | tf_op jit(solution)/shard_map/all_gather | solution.py:335
  872.1 20.0 %all-reduce.11 = (f32[960]{0:T(1024)S(1)}, f32[960]{0:T(1024)S(1)}) all-reduce(f32[960]{0:T(1024)S(1)} %get-tuple-element.372, f32[960]{0:T(1024)S(1)} %copy-done.29), channel_id=6, replica_groups=mesh['fsdp'=2,'context'=4,'tensor'=4] {'fsdp','context'}, use_global_device_ids=true, to_apply=%region_19.20.clone | all-reduce | flops 1920 | bytes 15360
  892.3 6.4 all-reduce.13
  899.1 8.9 all-reduce.14
  910.4 67.5 %all-reduce.18.cloned.1.call-done = (f32[960,80]{0,1:T(8,128)}, f32[960,80]{0,1:T(8,128)}) async-done(((f32[960,80]{0,1:T(8,128)}, f32[960,80]{0,1:T(8,128)}), (f32[960,80]{0,1:T(8,128)}, f32[960,80]{0,1:T(8,128)})) %all-reduce.18.cloned.1.call-update) | async-done | bytes 614416
  978.9 13.7 %all-gather.2 = f32[4,120,80]{1,2,0:T(8,128)S(1)} all-gather(f32[1,120,80]{1,2,0:T(8,128)S(1)} %dynamic-slice_bitcast_fusion.1), channel_id=1, replica_groups=mesh['fsdp'=2,'context'=4,'tensor'=4] {'context'}, dimensions={0}, use_global_device_ids=true | all-gather | bytes 192000 | tf_op jit(solution)/shard_map/all_gather | solution.py:329
  992.8 11.5 %all_gather.111 = f32[480,320]{0,1:T(8,128)S(1)} all-gather(f32[480,80]{0,1:T(8,128)S(1)} %reshape.169), channel_id=1, replica_groups=mesh['fsdp'=2,'context'=4,'tensor'=4] {'tensor'}, dimensions={1}, use_global_device_ids=true | all-gather | bytes 768000 | tf_op jit(solution)/shard_map/all_gather | solution.py:340
  1005.2 13.5 %all-gather.3 = f32[4,120,80]{1,2,0:T(8,128)S(1)} all-gather(f32[1,120,80]{1,2,0:T(8,128)S(1)} %dynamic-slice_bitcast_fusion), channel_id=1, replica_groups=mesh['fsdp'=2,'context'=4,'tensor'=4] {'context'}, dimensions={0}, use_global_device_ids=true | all-gather | bytes 192000 | tf_op jit(solution)/shard_map/all_gather | solution.py:330
  1018.9 11.6 %all_gather.113 = f32[480,320]{0,1:T(8,128)S(1)} all-gather(f32[480,80]{0,1:T(8,128)S(1)} %reshape.171), channel_id=1, replica_groups=mesh['fsdp'=2,'context'=4,'tensor'=4] {'tensor'}, dimensions={1}, use_global_device_ids=true | all-gather | bytes 768000 | tf_op jit(solution)/shard_map/all_gather | solution.py:341
  (355 shorter events, 196.1 us)
Async XLA Ops:
  7.2 62.9 %all-gather.19.cloned.1.call-start = ((), (), s32[]{:S(2)}) async-start(), calls=%async_computation.14 | async-start | bytes 2949120 | tf_op jit(solution)/shard_map/all_gather | solution.py:166
  7.9 27.4 %copy-start.33 = (s32[1,2048]{1,0:T(1,128)S(1)}, s32[1,2048]{1,0:T(1,128)}, u32[]{:S(2)}) copy-start(s32[1,2048]{1,0:T(1,128)} %param.19) | copy-start | bytes 24580
  7.9 27.6 %copy-start.3 = (bf16[128,960]{0,1:T(8,128)(2,1)S(1)}, bf16[128,960]{0,1:T(8,128)(2,1)}, u32[]{:S(2)}) copy-start(bf16[128,960]{0,1:T(8,128)(2,1)} %param.18) | copy-start | bytes 737284
  7.9 89.3 %all-gather.17.cloned.1.call-start = ((), (), s32[]{:S(2)}) async-start(), calls=%async_computation.13 | async-start | bytes 1392640 | tf_op jit(solution)/shard_map/all_gather | solution.py:188
  17.5 18.2 %copy-start.27 = (f32[960]{0:T(1024)}, f32[960]{0:T(1024)S(1)}, u32[]{:S(2)}) copy-start(f32[960]{0:T(1024)S(1)} %convert_element_type.95) | copy-start | bytes 11524
  35.3 18.7 %copy-start.5 = (bf16[960,320]{0,1:T(8,128)(2,1)}, bf16[960,320]{0,1:T(8,128)(2,1)S(1)}, u32[]{:S(2)}) copy-start(bf16[960,320]{0,1:T(8,128)(2,1)S(1)} %reshape.165) | copy-start | bytes 1843204
  35.5 37.1 %copy-start.20 = (f32[128,64]{0,1:T(8,128)}, f32[128,64]{0,1:T(8,128)S(1)}, u32[]{:S(2)}) copy-start(f32[128,64]{0,1:T(8,128)S(1)} %pad_maximum_fusion.3) | copy-start | bytes 98308
  35.7 19.0 %copy-start.36 = (f32[128]{0:T(128)}, f32[128]{0:T(128)S(1)}, u32[]{:S(2)}) copy-start(f32[128]{0:T(128)S(1)} %add_rsqrt_fusion.1) | copy-start | bytes 1540
  37.0 99.8 %all-gather.21.cloned.1.call-start = ((), (), s32[]{:S(2)}) async-start(), calls=%async_computation.15 | async-start | bytes 1392640 | tf_op jit(solution)/shard_map/all_gather | solution.py:189
  56.4 112.8 %all-gather.23.cloned.1.call-start = ((), (), s32[]{:S(2)}) async-start(), calls=%async_computation.16 | async-start | bytes 2949120 | tf_op jit(solution)/shard_map/all_gather | solution.py:169
  56.9 137.0 %all-gather.25.cloned.1.call-start = ((), (), s32[]{:S(2)}) async-start(), calls=%async_computation.17 | async-start | bytes 1843200 | tf_op jit(solution)/shard_map/all_gather | solution.py:170
  57.5 161.1 %all-gather.27.cloned.1.call-start = ((), (), s32[]{:S(2)}) async-start(), calls=%async_computation.18 | async-start | bytes 1843200 | tf_op jit(solution)/shard_map/all_gather | solution.py:171
  58.1 185.4 %all-gather.29.cloned.1.call-start = ((), (), s32[]{:S(2)}) async-start(), calls=%async_computation.19 | async-start | bytes 1843200 | tf_op jit(solution)/shard_map/all_gather | solution.py:172
  58.9 223.7 %reduce-scatter.20.cloned.1.call-start = ((), (), s32[]{:S(2)}) async-start(), calls=%async_computation.21 | async-start | bytes 2457600 | tf_op jit(solution)/shard_map/reduce_scatter | solution.py:236
  154.6 27.1 %copy-start.10 = (bf16[5,3,128,64]{2,3,1,0:T(8,128)(2,1)}, bf16[5,3,128,64]{2,3,1,0:T(8,128)(2,1)S(1)}, u32[]{:S(2)}) copy-start(bf16[5,3,128,64]{2,3,1,0:T(8,128)(2,1)S(1)} %convert_element_type.101) | copy-start | bytes 737284
  171.7 112.9 %copy-start.34 = (f32[128]{0:T(128)}, f32[128]{0:T(128)S(1)}, u32[]{:S(2)}) copy-start(f32[128]{0:T(128)S(1)} %add_rsqrt_fusion) | copy-start | bytes 1540
  252.0 238.7 %reduce-scatter.30.cloned.1.call-start = ((), (), s32[]{:S(2)}) async-start(), calls=%async_computation.31 | async-start | bytes 2764800
  255.6 235.8 %reduce-scatter.32.cloned.1.call-start = ((), (), s32[]{:S(2)}) async-start(), calls=%async_computation.32 | async-start | bytes 2764800
  259.2 244.0 %reduce-scatter.34.cloned.1.call-start = ((), (), s32[]{:S(2)}) async-start(), calls=%async_computation.33 | async-start | bytes 2764800
  262.7 23.8 %copy-start.2 = (bf16[960,960]{1,0:T(8,128)(2,1)S(1)}, bf16[960,960]{1,0:T(8,128)(2,1)}, u32[]{:S(2)}) copy-start(bf16[960,960]{1,0:T(8,128)(2,1)} %all-gather.23.cloned.1.call-done) | copy-start | bytes 5529604
  262.8 307.1 %reduce-scatter.22.cloned.1.call-start = ((), (), s32[]{:S(2)}) async-start(), calls=%async_computation.22 | async-start | bytes 2785280 | tf_op jit(solution)/shard_map/reduce_scatter | solution.py:263
  297.8 14.3 %copy-start.26 = (bf16[128,5,3,64]{0,3,2,1:T(8,128)(2,1)S(1)}, bf16[128,5,3,64]{0,3,2,1:T(8,128)(2,1)}, u32[]{:S(2)}) copy-start(bf16[128,5,3,64]{0,3,2,1:T(8,128)(2,1)} %get-tuple-element.726) | copy-start | bytes 737284 | tf_op jit(solution)/shard_map/while
  336.8 14.3 %copy-start.26 = (bf16[128,5,3,64]{0,3,2,1:T(8,128)(2,1)S(1)}, bf16[128,5,3,64]{0,3,2,1:T(8,128)(2,1)}, u32[]{:S(2)}) copy-start(bf16[128,5,3,64]{0,3,2,1:T(8,128)(2,1)} %get-tuple-element.726) | copy-start | bytes 737284 | tf_op jit(solution)/shard_map/while
  375.7 14.3 %copy-start.26 = (bf16[128,5,3,64]{0,3,2,1:T(8,128)(2,1)S(1)}, bf16[128,5,3,64]{0,3,2,1:T(8,128)(2,1)}, u32[]{:S(2)}) copy-start(bf16[128,5,3,64]{0,3,2,1:T(8,128)(2,1)} %get-tuple-element.726) | copy-start | bytes 737284 | tf_op jit(solution)/shard_map/while
  450.9 185.9 %reduce-scatter.24.cloned.1.call-start = ((), (), s32[]{:S(2)}) async-start(), calls=%async_computation.23 | async-start | bytes 2785280 | tf_op jit(solution)/shard_map/reduce_scatter | solution.py:264
  457.1 15.4 %all-to-all-start = ((bf16[128,4,240]{0,2,1:T(8,128)(2,1)}), bf16[128,4,240]{0,2,1:T(8,128)(2,1)S(1)}, u32[]{:S(2)}, u32[]{:S(2)}) async-start(bf16[128,4,240]{0,2,1:T(8,128)(2,1)} %add_convert_fusion), calls=%async_computation.4 | async-start | bytes 491520 | tf_op jit(solution)/shard_map/all_to_all | solution.py:296
  460.5 243.3 %reduce-scatter.26.cloned.1.call-start = ((), (), s32[]{:S(2)}) async-start(), calls=%async_computation.24 | async-start | bytes 1105920 | tf_op jit(solution)/shard_map/reduce_scatter | solution.py:316
  473.9 15.4 %all-to-all-start.3 = ((bf16[128,4,240]{0,2,1:T(8,128)(2,1)}), bf16[128,4,240]{0,2,1:T(8,128)(2,1)S(1)}, u32[]{:S(2)}, u32[]{:S(2)}) async-start(bf16[128,4,240]{0,2,1:T(8,128)(2,1)} %bitcast.34), calls=%async_computation.8 | async-start | bytes 491520 | tf_op jit(solution)/shard_map/all_to_all | solution.py:299
  477.3 293.4 %reduce-scatter.28.cloned.1.call-start = ((), (), s32[]{:S(2)}) async-start(), calls=%async_computation.26 | async-start | bytes 1105920 | tf_op jit(solution)/shard_map/reduce_scatter | solution.py:319
  490.7 313.5 %all-gather.35.cloned.1.call-start = ((), (), s32[]{:S(2)}) async-start(), calls=%async_computation.28 | async-start | bytes 1536000 | tf_op jit(solution)/shard_map/all_gather | solution.py:333
  491.3 344.3 %all-gather.37.cloned.1.call-start = ((), (), s32[]{:S(2)}) async-start(), calls=%async_computation.29 | async-start | bytes 1536000 | tf_op jit(solution)/shard_map/all_gather | solution.py:334
  491.9 375.5 %all-gather.39.cloned.1.call-start = ((), (), s32[]{:S(2)}) async-start(), calls=%async_computation.30 | async-start | bytes 1536000 | tf_op jit(solution)/shard_map/all_gather | solution.py:335
  503.2 404.9 %reduce-scatter.18.cloned.1.call-start = ((), (), s32[]{:S(2)}) async-start(), calls=%async_computation.20 | async-start | bytes 2457600 | tf_op jit(solution)/shard_map/reduce_scatter | solution.py:199
  572.4 66.1 %all-to-all-start.1 = ((bf16[128,4,80]{0,2,1:T(8,128)(2,1)}), bf16[128,4,80]{0,2,1:T(8,128)(2,1)S(1)}, u32[]{:S(2)}, u32[]{:S(2)}) async-start(bf16[128,4,80]{0,2,1:T(8,128)(2,1)} %bitcast.28), calls=%async_computation.6 | async-start | bytes 163840 | tf_op jit(solution)/shard_map/all_to_all | solution.py:297
  638.4 7.5 all-to-all-start.2
  641.7 336.2 %all-reduce.18.cloned.1.call-start = ((), (), s32[]{:S(2)}) async-start(), calls=%async_computation.34 | async-start | bytes 1310720
  647.1 142.6 %copy-start.42 = (u32[32]{0:T(128)S(1)}, u32[32]{0:T(128)}, u32[]{:S(2)}) copy-start(u32[32]{0:T(128)} %constant.104) | copy-start | bytes 388
  647.1 143.2 %copy-start.41 = (u32[32]{0:T(128)S(1)}, u32[32]{0:T(128)}, u32[]{:S(2)}) copy-start(u32[32]{0:T(128)} %constant.118) | copy-start | bytes 388
  647.1 383.4 %all-gather.31.cloned.1.call-start = ((), (), s32[]{:S(2)}) async-start(), calls=%async_computation.25 | async-start | bytes 2457600 | tf_op jit(solution)/shard_map/all_gather | solution.py:339
  721.1 312.2 %all-gather.33.cloned.1.call-start = ((), (), s32[]{:S(2)}) async-start(), calls=%async_computation.27 | async-start | bytes 2457600 | tf_op jit(solution)/shard_map/all_gather | solution.py:342
  789.6 80.9 %copy-start.1 = (bf16[960,960]{1,0:T(8,128)(2,1)S(1)}, bf16[960,960]{1,0:T(8,128)(2,1)}, u32[]{:S(2)}) copy-start(bf16[960,960]{1,0:T(8,128)(2,1)} %all-gather.19.cloned.1.call-done) | copy-start | bytes 5529604
  789.7 80.9 %copy-start.4 = (bf16[128,960]{0,1:T(8,128)(2,1)S(1)}, bf16[128,960]{0,1:T(8,128)(2,1)}, u32[]{:S(2)}) copy-start(bf16[128,960]{0,1:T(8,128)(2,1)} %param.18) | copy-start | bytes 737284
  789.7 80.9 %copy-start.28 = (f32[960]{0:T(1024)S(1)}, f32[960]{0:T(1024)}, u32[]{:S(2)}) copy-start(f32[960]{0:T(1024)} %copy-done.27) | copy-start | bytes 11524
  789.7 80.9 %copy-start.37 = (f32[128]{0:T(128)S(1)}, f32[128]{0:T(128)}, u32[]{:S(2)}) copy-start(f32[128]{0:T(128)} %copy-done.36) | copy-start | bytes 1540
  870.6 37.5 %copy-start.7 = (f32[128,960]{0,1:T(8,128)S(1)}, f32[128,960]{0,1:T(8,128)}, u32[]{:S(2)}) copy-start(f32[128,960]{0,1:T(8,128)} %reduce-scatter.20.cloned.1.call-done) | copy-start | bytes 1474564
  870.6 37.5 %copy-start.14 = (bf16[128,960]{0,1:T(8,128)(2,1)S(1)}, bf16[128,960]{0,1:T(8,128)(2,1)}, u32[]{:S(2)}) copy-start(bf16[128,960]{0,1:T(8,128)(2,1)} %param.20) | copy-start | bytes 737284
  870.6 37.5 %copy-start.35 = (f32[128]{0:T(128)S(1)}, f32[128]{0:T(128)}, u32[]{:S(2)}) copy-start(f32[128]{0:T(128)} %copy-done.34) | copy-start | bytes 1540
  870.6 37.5 %copy-start.39 = (f32[128]{0:T(128)S(1)}, f32[128]{0:T(128)}, u32[]{:S(2)}) copy-start(f32[128]{0:T(128)} %copy-done.38) | copy-start | bytes 1540
  (39 other events, 156.5 us)
Sparse Core Ops, SparseCore 0:
  9.5 45.8 all-gather.18
  58.1 39.1 all-gather.16
  100.0 36.8 all-gather.20
  138.3 30.9 all-gather.22
  170.6 23.2 all-gather.24
  195.3 23.2 all-gather.26
  220.2 23.2 all-gather.28
  252.1 30.3 reduce-scatter.19
  286.2 70.8 reduce-scatter.29
  360.6 69.2 reduce-scatter.31
  433.5 69.6 reduce-scatter.33
  506.8 62.9 reduce-scatter.21
  573.6 63.2 reduce-scatter.23
  640.6 63.1 reduce-scatter.25
  707.5 63.1 reduce-scatter.27
  772.2 31.9 all-gather.34
  805.6 29.9 all-gather.36
  837.0 30.2 all-gather.38
  870.5 29.7 reduce-scatter.17
  904.1 73.7 all-reduce.17
  980.1 24.7 all-gather.30
  1007.0 25.3 all-gather.32
where the time goes:
time: 1060 us; the launch traced here: 1050 us
  waiting for transfers between devices  508 us (48%)
  blocking collectives  203 us (19%)
  local copies, waits for them, and re-layouts  162 us (15%)
  matrix products  111 us (10%)
  other arithmetic  31.1 us (3%)
  between operations  17.3 us (2%)
  starting transfers between devices  14.7 us (1%)
    dynamic_update_slice x16, local copies, waits for them, and re-layouts, attend_backward(): d_query, (d_keys, d_values) = lax.scan(step, start, blocks)  114 us
    unnamed x26, waiting for transfers between devices  83 us
    reduce_scatter x1, waiting for transfers between devices, per_device(): lax.psum_scatter(key_terms, ('context', 'tensor'), scatter_dimension=0, t...  62.6 us
    reduce_scatter x1, waiting for transfers between devices, per_device(): lax.psum_scatter(value_terms, ('context', 'tensor'), scatter_dimension=0,...  61.2 us
    reduce_scatter x1, waiting for transfers between devices, per_device(): lax.psum_scatter(query_grad, ('fsdp', 'context'), scatter_dimension=0, ti...  56.6 us
    reduce_scatter x1, waiting for transfers between devices, per_device(): lax.psum_scatter(out_grad, ('fsdp', 'context'), scatter_dimension=0, tile...  49.6 us
    unnamed x105, local copies, waits for them, and re-layouts  36 us
    unnamed x3, blocking collectives  34.8 us
  transfers between devices with their start and end apart: 26, of which 17 were waited for; matrix products, arithmetic and copies ran while one was open for 27% of the time, Pallas kernels for 0%

commit v1 on v0

v1 whole, which is shorter than its diff:
```python
import jax
import jax.numpy as jnp
from jax import lax
from jax.experimental import pallas as pl
from jax.experimental.pallas import tpu as pltpu
from jax.sharding import PartitionSpec as P

HEADS = 15
KV_HEADS = 5
HD = 64


EPS = 1e-05
THETA = 100000.0
NEG = -1e30
ROWS_MATCH = (((0,), (0,)), ((), ()))
COLS_MATCH = (((1,), (1,)), ((), ()))


def norm_scale(values):
    return lax.rsqrt(jnp.mean(values * values, axis=1, keepdims=True) + EPS)


def norm_back(grad, hat, scale, gain):
    weighted = grad * gain
    return scale * (weighted - hat * jnp.mean(weighted * hat, axis=1, keepdims=True))


def rotary_tables(places):
    half = HD // 2
    freq = THETA ** (-2.0 * jnp.arange(half, dtype=jnp.float32) / HD)
    angle = places.astype(jnp.float32)[:, None] * freq[None, :]
    cosine = jnp.concatenate([jnp.cos(angle), jnp.cos(angle)], axis=1)[:, None, :]
    sine = jnp.concatenate([jnp.sin(angle), jnp.sin(angle)], axis=1)[:, None, :]
    return (cosine, sine)


def rotate(values, cosine, sine):
    half = values.shape[-1] // 2
    turned = jnp.concatenate([-values[..., half:], values[..., :half]], axis=-1)
    return values * cosine + turned * sine


def unrotate(values, cosine, sine):
    half = values.shape[-1] // 2
    scaled = values * sine
    return values * cosine + jnp.concatenate([scaled[..., half:], -scaled[..., :half]], axis=-1)


KEYS_MATCH = (((0,), (0,)), ((), ()))


def masked_scores(kv, queries, key_places, own_places):
    scores = lax.dot_general(
        kv, queries, COLS_MATCH, preferred_element_type=jnp.float32
    ) * HD ** (-0.5)
    return jnp.where(key_places <= own_places, scores, NEG)


def forward_kernel(key_places_ref, own_places_ref, q_ref, kv_ref, out_ref, lse_ref):
    owners, _, block, width = kv_ref.shape
    kv = kv_ref[...].reshape(owners * block, width)
    scores = masked_scores(kv, q_ref[0], key_places_ref[...], own_places_ref[...])
    peak = jnp.max(scores, axis=0, keepdims=True)
    weights = jnp.exp(scores - peak)
    summed = jnp.sum(weights, axis=0, keepdims=True)
    mixed = lax.dot_general(
        kv, weights.astype(jnp.bfloat16), KEYS_MATCH, preferred_element_type=jnp.float32
    )
    out_ref[0] = (mixed[HD:] / summed).astype(jnp.bfloat16)
    lse_ref[0] = peak + jnp.log(summed)


def backward_kernel(
    key_places_ref, own_places_ref, q_ref, d_att_ref, kv_ref, lse_ref, delta_ref, dq_ref, dkv_ref
):
    owners, _, block, width = kv_ref.shape
    kv = kv_ref[...].reshape(owners * block, width)
    scores = masked_scores(kv, q_ref[0], key_places_ref[...], own_places_ref[...])
    probs = jnp.exp(scores - lse_ref[0])
    d_probs = lax.dot_general(kv, d_att_ref[0], COLS_MATCH, preferred_element_type=jnp.float32)
    d_scores = (probs * (d_probs - delta_ref[0]) * HD ** (-0.5)).astype(jnp.bfloat16)
    dq = lax.dot_general(kv, d_scores, KEYS_MATCH, preferred_element_type=jnp.float32)
    dq_ref[0] = dq[:HD]
    d_kv = jnp.dot(d_scores, q_ref[0], preferred_element_type=jnp.float32)
    d_kv = d_kv + jnp.dot(
        probs.astype(jnp.bfloat16), d_att_ref[0], preferred_element_type=jnp.float32
    )
    dkv_ref[...] = d_kv.astype(jnp.bfloat16).reshape(owners, 1, block, width)


def attention_specs(all_kv, lanes):
    owners, _, block, width = all_kv.shape
    total = owners * block
    places = pl.BlockSpec((total, 1), lambda g: (0, 0))
    own = pl.BlockSpec((1, lanes), lambda g: (0, 0))
    queries = pl.BlockSpec((1, lanes, width), lambda g: (g, 0, 0))
    kv = pl.BlockSpec((owners, 1, block, width), lambda g: (0, g, 0, 0))
    row = pl.BlockSpec((1, 1, lanes), lambda g: (g, 0, 0))
    turned = pl.BlockSpec((1, HD, lanes), lambda g: (g, 0, 0))
    cost = KV_HEADS * total * lanes
    return places, own, queries, kv, row, turned, cost


def attend_forward(key_places, own_lanes, q_pad, all_kv):
    lanes = q_pad.shape[1]
    places, own, queries, kv, row, turned, cost = attention_specs(all_kv, lanes)
    return pl.pallas_call(
        forward_kernel,
        grid=(KV_HEADS,),
        in_specs=[places, own, queries, kv],
        out_specs=[turned, row],
        out_shape=[
            jax.ShapeDtypeStruct((KV_HEADS, HD, lanes), jnp.bfloat16),
            jax.ShapeDtypeStruct((KV_HEADS, 1, lanes), jnp.float32),
        ],
        cost_estimate=pl.CostEstimate(
            flops=8 * HD * cost, bytes_accessed=2 * all_kv.size, transcendentals=cost
        ),
    )(key_places, own_lanes, q_pad, all_kv)


def attend_backward(key_places, own_lanes, q_pad, d_att_pad, all_kv, totals, delta):
    lanes = q_pad.shape[1]
    places, own, queries, kv, row, turned, cost = attention_specs(all_kv, lanes)
    return pl.pallas_call(
        backward_kernel,
        grid=(KV_HEADS,),
        in_specs=[places, own, queries, queries, kv, row, row],
        out_specs=[turned, kv],
        out_shape=[
            jax.ShapeDtypeStruct((KV_HEADS, HD, lanes), jnp.float32),
            jax.ShapeDtypeStruct(all_kv.shape, jnp.bfloat16),
        ],
        cost_estimate=pl.CostEstimate(
            flops=20 * HD * cost, bytes_accessed=4 * all_kv.size, transcendentals=cost
        ),
    )(key_places, own_lanes, q_pad, d_att_pad, all_kv, totals, delta)


def per_device(
    tokens,
    positions,
    cotangent,
    attn_gain,
    query_weight,
    key_weight,
    value_weight,
    out_weight,
    mlp_gain,
    gate_weight,
    up_weight,
    down_weight,
):
    rows, width = tokens.shape
    groups = HEADS // KV_HEADS
    lanes = groups * rows
    q_cols, kv_cols = query_weight.shape[1], key_weight.shape[1]
    qkv_cols = q_cols + 2 * kv_cols
    hidden = gate_weight.shape[1]
    place = lax.axis_index(("context", "tensor"))
    sequence_places = positions[0]
    own_places = lax.dynamic_slice_in_dim(sequence_places, place * rows, rows, 0)
    key_places = sequence_places[:, None]
    own_lanes = jnp.tile(own_places, groups)[None, :]

    first_pack = lax.all_gather(
        jnp.concatenate(
            [query_weight, key_weight, value_weight, attn_gain[:, None], mlp_gain[:, None]], axis=1
        ),
        "fsdp",
        axis=0,
        tiled=True,
    )
    qkv_full = first_pack[:, :qkv_cols]
    gain_one = first_pack[:, qkv_cols].astype(jnp.float32)
    gain_two = first_pack[:, qkv_cols + 1].astype(jnp.float32)
    second_pack = lax.all_gather(
        jnp.concatenate([gate_weight, up_weight, down_weight, out_weight], axis=1),
        "fsdp",
        axis=0,
        tiled=True,
    )
    gate_up_full = second_pack[:, : 2 * hidden]
    down_full = second_pack[:, 2 * hidden : 3 * hidden]
    out_full = second_pack[:, 3 * hidden :]

    inputs = tokens.astype(jnp.float32)
    first_scale = norm_scale(inputs)
    normed_one = (inputs * first_scale * gain_one).astype(jnp.bfloat16)
    cosine, sine = rotary_tables(own_places)
    qkv = jnp.dot(normed_one, qkv_full, preferred_element_type=jnp.float32)
    query = qkv[:, :q_cols].reshape(rows, HEADS, HD)
    key_raw = qkv[:, q_cols : q_cols + kv_cols].reshape(rows, KV_HEADS, HD)
    value = qkv[:, q_cols + kv_cols :].reshape(rows, KV_HEADS, HD).astype(jnp.bfloat16)
    q_rot = rotate(query, cosine, sine).astype(jnp.bfloat16)
    k_rot = rotate(key_raw, cosine, sine).astype(jnp.bfloat16)
    own_kv = jnp.transpose(jnp.concatenate([k_rot, value], axis=2), (1, 0, 2))
    all_kv = lax.all_gather(own_kv, ("context", "tensor"), axis=0)
    q_group = jnp.transpose(q_rot, (1, 0, 2)).reshape(KV_HEADS, lanes, HD)
    q_pad = jnp.pad(q_group, ((0, 0), (0, 0), (0, HD)))
    turned, totals = attend_forward(key_places, own_lanes, q_pad, all_kv)
    attended = jnp.transpose(
        turned.reshape(KV_HEADS, HD, groups, rows), (3, 0, 2, 1)
    ).reshape(rows, HEADS * HD)

    residual = inputs + jnp.dot(attended, out_full, preferred_element_type=jnp.float32)
    second_scale = norm_scale(residual)
    hat_two = residual * second_scale
    normed_two = (hat_two * gain_two).astype(jnp.bfloat16)
    mlp_rows = lax.all_gather(normed_two, "tensor", axis=0, tiled=True)
    cot_rows = lax.all_gather(cotangent, "tensor", axis=0, tiled=True)
    gate_up = jnp.dot(mlp_rows, gate_up_full, preferred_element_type=jnp.float32)
    gate, up = gate_up[:, :hidden], gate_up[:, hidden:]
    sig = jax.nn.sigmoid(gate)
    act = (gate * sig * up).astype(jnp.bfloat16)
    d_act = jnp.dot(cot_rows, down_full, preferred_element_type=jnp.float32)
    d_gate = (d_act * up * sig * (1.0 + gate * (1.0 - sig))).astype(jnp.bfloat16)
    d_up = (d_act * gate * sig).astype(jnp.bfloat16)
    d_gate_up = jnp.concatenate([d_gate, d_up], axis=1)
    d_normed_two = lax.psum_scatter(
        lax.dot_general(
            d_gate_up, gate_up_full, COLS_MATCH, preferred_element_type=jnp.float32
        ).astype(jnp.bfloat16),
        "tensor",
        scatter_dimension=0,
        tiled=True,
    ).astype(jnp.float32)
    feed = lax.psum_scatter(
        lax.dot_general(act, down_full, COLS_MATCH, preferred_element_type=jnp.float32).astype(
            jnp.bfloat16
        ),
        "tensor",
        scatter_dimension=0,
        tiled=True,
    )
    output = (residual + feed.astype(jnp.float32)).astype(jnp.bfloat16)
    mlp_grads = jnp.concatenate(
        [
            lax.dot_general(mlp_rows, d_gate_up, ROWS_MATCH, preferred_element_type=jnp.float32),
            lax.dot_general(cot_rows, act, ROWS_MATCH, preferred_element_type=jnp.float32),
        ],
        axis=1,
    ).astype(jnp.bfloat16)

    mlp_gain_grad = jnp.sum(d_normed_two * hat_two, axis=0)
    d_residual = cotangent.astype(jnp.float32) + norm_back(
        d_normed_two, hat_two, second_scale, gain_two
    )
    residual_round = d_residual.astype(jnp.bfloat16)
    d_attended = lax.dot_general(
        residual_round, out_full, COLS_MATCH, preferred_element_type=jnp.float32
    ).astype(jnp.bfloat16)
    delta = jnp.sum(
        (d_attended.astype(jnp.float32) * attended.astype(jnp.float32)).reshape(rows, HEADS, HD),
        axis=-1,
    )
    delta = jnp.transpose(delta).reshape(KV_HEADS, 1, lanes)
    d_att_group = jnp.transpose(d_attended.reshape(rows, HEADS, HD), (1, 0, 2))
    d_att_pad = jnp.pad(d_att_group.reshape(KV_HEADS, lanes, HD), ((0, 0), (0, 0), (HD, 0)))
    dq_turned, dkv_terms = attend_backward(
        key_places, own_lanes, q_pad, d_att_pad, all_kv, totals, delta
    )
    own_dkv = lax.psum_scatter(dkv_terms, ("context", "tensor"), scatter_dimension=0)
    own_dkv = jnp.transpose(own_dkv.astype(jnp.float32), (1, 0, 2))
    d_query = jnp.transpose(dq_turned.reshape(KV_HEADS, HD, groups, rows), (3, 0, 2, 1)).reshape(
        rows, HEADS, HD
    )
    dq_rot = unrotate(d_query, cosine, sine).astype(jnp.bfloat16).reshape(rows, q_cols)
    dk_rot = unrotate(own_dkv[..., :HD], cosine, sine).astype(jnp.bfloat16).reshape(rows, kv_cols)
    dv_round = own_dkv[..., HD:].astype(jnp.bfloat16).reshape(rows, kv_cols)
    d_qkv = jnp.concatenate([dq_rot, dk_rot, dv_round], axis=1)
    d_normed_one = lax.dot_general(
        d_qkv, qkv_full, COLS_MATCH, preferred_element_type=jnp.float32
    )
    hat_one = inputs * first_scale
    attn_gain_grad = jnp.sum(d_normed_one * hat_one, axis=0)
    input_grad = d_residual + norm_back(d_normed_one, hat_one, first_scale, gain_one)

    parts = lax.axis_size("tensor")
    gathered_rows = lax.all_gather(
        jnp.concatenate([normed_one, attended], axis=1), "tensor", axis=0, tiled=True
    )
    quarters = jnp.concatenate(
        [
            piece.reshape(rows, parts, piece.shape[1] // parts)
            for piece in (dq_rot, dk_rot, dv_round, residual_round)
        ],
        axis=2,
    )
    own_cols = lax.all_to_all(quarters, "tensor", split_axis=1, concat_axis=0, tiled=True)
    own_cols = own_cols.reshape(parts * rows, quarters.shape[2])
    cut = qkv_cols // parts
    attn_grads = jnp.concatenate(
        [
            lax.dot_general(
                gathered_rows[:, :width],
                own_cols[:, :cut],
                ROWS_MATCH,
                preferred_element_type=jnp.float32,
            ),
            lax.dot_general(
                gathered_rows[:, width:],
                own_cols[:, cut:],
                ROWS_MATCH,
                preferred_element_type=jnp.float32,
            ),
            attn_gain_grad[:, None],
            mlp_gain_grad[:, None],
        ],
        axis=1,
    ).astype(jnp.bfloat16)

    mlp_share = lax.psum_scatter(
        mlp_grads, ("fsdp", "context"), scatter_dimension=0, tiled=True
    )
    mlp_owned = lax.all_gather(mlp_share, "context", axis=0, tiled=True).astype(jnp.float32)
    attn_share = lax.psum_scatter(
        attn_grads, ("fsdp", "context"), scatter_dimension=0, tiled=True
    )
    pieces = lax.all_gather(attn_share, ("context", "tensor"), axis=0)
    pieces = pieces.reshape(
        lax.axis_size("context"), parts, pieces.shape[1], pieces.shape[2]
    ).astype(jnp.float32)

    def whole(start, count):
        part = jnp.transpose(pieces[..., start : start + count], (0, 2, 1, 3))
        return part.reshape(part.shape[0] * part.shape[1], parts * count)

    q_part, kv_part = q_cols // parts, kv_cols // parts
    gains = jnp.sum(pieces[..., cut + width // parts :], axis=1).reshape(-1, 2)
    return (
        output,
        input_grad,
        gains[:, 0],
        whole(0, q_part),
        whole(q_part, kv_part),
        whole(q_part + kv_part, kv_part),
        whole(cut, width // parts),
        gains[:, 1],
        mlp_owned[:, :hidden],
        mlp_owned[:, hidden : 2 * hidden],
        mlp_owned[:, 2 * hidden :],
    )


def solution(mesh):
    return jax.shard_map(
        per_device,
        mesh=mesh,
        in_specs=(
            P(("fsdp", "context", "tensor"), None),
            P("fsdp", None),
            P(("fsdp", "context", "tensor"), None),
            P("fsdp"),
            P("fsdp", None),
            P("fsdp", None),
            P("fsdp", None),
            P("fsdp", None),
            P("fsdp"),
            P("fsdp", "tensor"),
            P("fsdp", "tensor"),
            P("fsdp", "tensor"),
        ),
        out_specs=(
            P(("fsdp", "context", "tensor"), None),
            P(("fsdp", "context", "tensor"), None),
            P("fsdp"),
            P("fsdp", None),
            P("fsdp", None),
            P("fsdp", None),
            P("fsdp", None),
            P("fsdp"),
            P("fsdp", "tensor"),
            P("fsdp", "tensor"),
            P("fsdp", "tensor"),
        ),
        check_vma=False,
    )
```

time: 1060 us -> 649 us (0.61)
  blocking collectives: 203 us -> 21.8 us
  local copies, waits for them, and re-layouts: 162 us -> 52.8 us
  matrix products: 111 us -> 30 us
  waiting for transfers between devices: 508 us -> 482 us
  Pallas kernels: 0 us -> 25.1 us
  other arithmetic: 31.1 us -> 17.4 us
    reduce_scatter x6 -> x1, waiting for transfers between devices: 250 us -> 54.9 us  [per_device(): lax.psum_scatter(dkv_terms, ('context', 'tensor'), scatter_dimension=0)]
    all_gather x10 -> x0, blocking collectives: 142 us -> none  [the longest x1 17.9 us: per_device(): lax.all_gather(merged[4], 'context', axis=0, tiled=True)]
    dynamic_update_slice x16 -> x0, local copies, waits for them, and re-layouts: 114 us -> none  [attend_backward(): d_query, (d_keys, d_values) = lax.scan(step, start, blocks)]
    unnamed x26 -> x15, waiting for transfers between devices: 83 us -> 191 us
    dot_general x44 -> x7, matrix products: 95.8 us -> 17.3 us  [the longest x1 3.41 us: per_device(): jnp.dot(mlp_rows, gate_up_full, preferred_element_type=jnp.float32)]
    all_gather x12 -> x6, waiting for transfers between devices: 173 us -> 222 us  [the longest x1 62.2 us: per_device(): lax.all_gather(jnp.concatenate([gate_weight, up_weight, down_weight, out_...]
    unnamed x3 -> x0, blocking collectives: 34.8 us -> none
    pallas_call x0 -> x2, Pallas kernels: none -> 25.1 us  [the longest x1 14.8 us: attend_backward(): pl.pallas_call(backward_kernel, grid=(KV_HEADS,), in_specs=[places, own,...]
  transfers between devices with their start and end apart: 26 -> 12, of which waited for: 17 -> 12; matrix products, arithmetic and copies ran while one was open for 27% -> 6% of each run, Pallas kernels for 0% -> 2%
where the time goes in v1:
time: 649 us; the launch traced here: 647 us
  waiting for transfers between devices  482 us (74%)
  local copies, waits for them, and re-layouts  52.8 us (8%)
  matrix products  30 us (5%)
  Pallas kernels  25.1 us (4%)
  blocking collectives  21.8 us (3%)
  other arithmetic  17.4 us (3%)
  between operations  14.5 us (2%)
    unnamed x15, waiting for transfers between devices  191 us
    all_gather x1, waiting for transfers between devices, per_device(): lax.all_gather(jnp.concatenate([gate_weight, up_weight, down_weight, out_...  62.2 us
    reduce_scatter x1, waiting for transfers between devices, per_device(): lax.psum_scatter(dkv_terms, ('context', 'tensor'), scatter_dimension=0)  54.9 us
    all_gather x1, waiting for transfers between devices, per_device(): lax.all_gather(jnp.concatenate([query_weight, key_weight, value_weight, a...  47.7 us
    all_gather x1, waiting for transfers between devices, per_device(): pieces = lax.all_gather(attn_share, ('context', 'tensor'), axis=0)  41.2 us
    all_gather x1, waiting for transfers between devices, per_device(): lax.all_gather(mlp_share, 'context', axis=0, tiled=True).astype(jnp.float32)  40.5 us
    all_gather x1, waiting for transfers between devices, per_device(): all_kv = lax.all_gather(own_kv, ('context', 'tensor'), axis=0)  26.2 us
    unnamed x68, local copies, waits for them, and re-layouts  16.5 us
  transfers between devices with their start and end apart: 12, of which 12 were waited for; matrix products, arithmetic and copies ran while one was open for 6% of the time, Pallas kernels for 2%

profile of v1, /device:TPU:0, one launch (start us, length us, event | category | flops | bytes accessed | tf_op | source)
XLA Modules:
  0.0 647.4 jit_solution(12713653227136648879)
XLA Ops:
  7.2 1.2 copy.119
  8.4 1.2 copy.120
  11.3 3.7 concatenate.51
  15.8 47.7 %all-gather.10.cloned.1.call-done = bf16[960,1602]{1,0:T(8,128)(2,1)} async-done(((bf16[480,1602]{1,0:T(8,128)(2,1)}), bf16[960,1602]{1,0:T(8,128)(2,1)}) %all-gather.10.cloned.1.call-update) | async-done | bytes 3075856 | tf_op jit(solution)/shard_map/all_gather | solution.py:167
  63.4 1.4 convert_reduce_fusion
  65.1 3.4 fusion.2
  70.9 2.7 pad_maximum_fusion.1
  73.9 1.4 copy.130.key_places_ref
  75.8 11.9 %all_gather.35 = bf16[512,960]{0,1:T(8,128)(2,1)} all-gather(bf16[128,960]{0,1:T(8,128)(2,1)S(1)} %copy-done), channel_id=1, replica_groups=mesh['fsdp'=2,'context'=4,'tensor'=4] {'tensor'}, dimensions={0}, use_global_device_ids=true | all-gather | bytes 1228800 | tf_op jit(solution)/shard_map/all_gather | solution.py:212
  89.0 26.2 %all-gather.18.cloned.1.call-done = bf16[80,128,128]{2,1,0:T(8,128)(2,1)} async-done(((bf16[5,128,128]{2,1,0:T(8,128)(2,1)}), bf16[80,128,128]{2,1,0:T(8,128)(2,1)}) %all-gather.18.cloned.1.call-update) | async-done | bytes 2621456 | tf_op jit(solution)/shard_map/all_gather | solution.py:199
  115.3 10.3 %shard_map.203 = (bf16[5,64,384]{2,1,0:T(8,128)(2,1)}, f32[5,1,384]{2,1,0:T(1,128)}) custom-call(s32[2048,1]{1,0:T(8,128)} %copy.130.key_places_ref, s32[1,384]{1,0:T(1,128)} %bitcast.124, bf16[5,384,128]{2,1,0:T(8,128)(2,1)} %pad.8.q_ref, bf16[16,5,128,128]{3,2,1,0:T(8,128)(2,1)} %bitcast.126), custom_call_target="tpu_custom_call" | custom-call | flops 2013265920 | bytes 2621440 | tf_op jit(solution)/shard_map/pallas_call | solution.py:108
  126.6 62.2 %all-gather.12.cloned.1.call-done = bf16[960,2880]{1,0:T(8,128)(2,1)} async-done(((bf16[480,2880]{1,0:T(8,128)(2,1)}), bf16[960,2880]{1,0:T(8,128)(2,1)}) %all-gather.12.cloned.1.call-update) | async-done | bytes 5529616 | tf_op jit(solution)/shard_map/all_gather | solution.py:178
  188.8 2.4 multiply_reduce_fusion
  191.5 10.0 %all_gather.34 = bf16[512,960]{0,1:T(8,128)(2,1)S(1)} all-gather(bf16[128,960]{0,1:T(8,128)(2,1)S(1)} %multiply_convert_fusion.3), channel_id=1, replica_groups=mesh['fsdp'=2,'context'=4,'tensor'=4] {'tensor'}, dimensions={0}, use_global_device_ids=true | all-gather | bytes 1228800 | tf_op jit(solution)/shard_map/all_gather | solution.py:211
  201.5 3.4 fusion.6
  204.9 2.4 multiply_convert_fusion.1
  208.3 2.4 fusion.12
  210.7 2.3 copy.151
  213.1 24.4 %reduce-scatter.18.cloned.1.call-done = bf16[128,960]{1,0:T(8,128)(2,1)} async-done(((bf16[512,960]{1,0:T(8,128)(2,1)}), bf16[128,960]{1,0:T(8,128)(2,1)}) %reduce-scatter.18.cloned.1.call-update) | async-done | bytes 245776
  239.8 3.1 convert_multiply_fusion.4
  246.7 14.8 %shard_map.204 = (f32[5,64,384]{2,1,0:T(8,128)}, bf16[16,5,128,128]{3,2,1,0:T(8,128)(2,1)}) custom-call(s32[2048,1]{1,0:T(8,128)} %copy.130.key_places_ref, s32[1,384]{1,0:T(1,128)} %bitcast.125, bf16[5,384,128]{2,1,0:T(8,128)(2,1)} %pad.8.q_ref, bf16[5,384,128]{2,1,0:T(8,128)(2,1)} %pad.9.d_att_ref, bf16[16,5,128,128]{3,2,1,0:T(8,128)(2,1)} %bitcast.127, ...), custom_call_target="tpu_custom_call" | custom-call | flops 5033164800 | bytes 5242880 | tf_op jit(solution)/shard_map/pallas_call | solution.py:126
  263.4 2.4 fusion.15
  265.9 1.4 convolution_convert_fusion
  267.3 2.2 pad_maximum_fusion
  271.1 54.9 %reduce-scatter.14.cloned.1.call-done = bf16[1,5,128,128]{3,2,1,0:T(8,128)(2,1)} async-done(((bf16[16,5,128,128]{3,2,1,0:T(8,128)(2,1)}), bf16[1,5,128,128]{3,2,1,0:T(8,128)(2,1)}) %reduce-scatter.14.cloned.1.call-update) | async-done | bytes 163856 | tf_op jit(solution)/shard_map/reduce_scatter | solution.py:264
  330.6 3.5 all-to-all-start
  335.1 3.1 fusion.42
  338.2 13.3 %all-to-all-done = bf16[128,4,640]{0,2,1:T(8,128)(2,1)S(1)} async-done(((bf16[128,4,640]{0,2,1:T(8,128)(2,1)}), bf16[128,4,640]{0,2,1:T(8,128)(2,1)S(1)}, u32[]{:S(2)}, u32[]{:S(2)}) %all-to-all-start) | async-done | bytes 655392 | tf_op jit(solution)/shard_map/all_to_all | solution.py:291
  351.8 4.3 all-gather.14.cloned.1.call-done
  356.1 1.7 convolution_convert_fusion.4
  357.8 1.8 convolution_convert_fusion.3
  359.8 1.6 copy.153
  361.5 2.4 convolution_convert_fusion.2
  364.0 1.3 copy.149
  365.4 74.2 %reduce-scatter.22.cloned.1.call-done = bf16[120,1920]{1,0:T(8,128)(2,1)} async-done(((bf16[960,1920]{1,0:T(8,128)(2,1)}), bf16[120,1920]{1,0:T(8,128)(2,1)}) %reduce-scatter.22.cloned.1.call-update) | async-done | bytes 460816
  439.7 67.2 %reduce-scatter.20.cloned.1.call-done = bf16[120,642]{1,0:T(8,128)(2,1)} async-done(((bf16[960,642]{1,0:T(8,128)(2,1)}), bf16[120,642]{1,0:T(8,128)(2,1)}) %reduce-scatter.20.cloned.1.call-update) | async-done | bytes 154096
  506.9 1.7 copy.154
  508.6 25.3 %reduce-scatter.16.cloned.1.call-done = bf16[128,960]{1,0:T(8,128)(2,1)} async-done(((bf16[512,960]{1,0:T(8,128)(2,1)}), bf16[128,960]{1,0:T(8,128)(2,1)}) %reduce-scatter.16.cloned.1.call-update) | async-done | bytes 245776
  536.3 40.5 %all-gather.16.cloned.1.call-done = bf16[480,1920]{1,0:T(8,128)(2,1)} async-done(((bf16[120,1920]{1,0:T(8,128)(2,1)}), bf16[480,1920]{1,0:T(8,128)(2,1)}) %all-gather.16.cloned.1.call-update) | async-done | bytes 1843216 | tf_op jit(solution)/shard_map/all_gather | solution.py:317
  576.8 3.4 fusion.63
  580.2 41.2 %all-gather.20.cloned.1.call-done = bf16[16,120,642]{1,2,0:T(8,128)(2,1)} async-done(((bf16[1,120,642]{1,2,0:T(8,128)(2,1)}), bf16[16,120,642]{1,2,0:T(8,128)(2,1)}) %all-gather.20.cloned.1.call-update) | async-done | bytes 2465296 | tf_op jit(solution)/shard_map/all_gather | solution.py:321
  621.4 2.1 bitcast_convert_fusion
  623.5 2.2 slice_bitcast_fusion
  627.4 2.0 copy.144
  629.4 2.6 reshape.171
  632.0 1.5 copy.145
  636.3 2.0 copy.147
  638.3 2.6 reshape.174
  (148 shorter events, 31.9 us)
Async XLA Ops:
  7.2 56.2 %all-gather.10.cloned.1.call-start = ((), (), s32[]{:S(2)}) async-start(), calls=%async_computation.6 | async-start | bytes 4792320 | tf_op jit(solution)/shard_map/all_gather | solution.py:167
  11.3 3.9 copy-start.18
  11.3 4.3 copy-start.1
  15.1 100.2 %all-gather.18.cloned.1.call-start = ((), (), s32[]{:S(2)}) async-start(), calls=%async_computation.11 | async-start | bytes 2785280 | tf_op jit(solution)/shard_map/all_gather | solution.py:199
  15.8 52.7 %copy-start.21 = (f32[128]{0:T(128)}, f32[128]{0:T(128)S(1)}, u32[]{:S(2)}) copy-start(f32[128]{0:T(128)S(1)} %add_rsqrt_fusion.1) | copy-start | bytes 1540
  64.9 3.6 copy-start.16
  64.9 174.7 %copy-start.14 = (f32[960]{0:T(1024)}, f32[960]{0:T(1024)S(1)}, u32[]{:S(2)}) copy-start(f32[960]{0:T(1024)S(1)} %get-tuple-element.19) | copy-start | bytes 11524
  68.5 0.9 copy-start.8
  68.5 2.4 copy-start.5
  68.5 2.4 copy-start.10
  70.9 118.0 %all-gather.12.cloned.1.call-start = ((), (), s32[]{:S(2)}) async-start(), calls=%async_computation.7 | async-start | bytes 8478720 | tf_op jit(solution)/shard_map/all_gather | solution.py:178
  73.7 2.2 copy-start
  73.7 14.0 %copy-start.9 = (f32[128,1600]{0,1:T(8,128)S(1)}, f32[128,1600]{0,1:T(8,128)}, u32[]{:S(2)}) copy-start(f32[128,1600]{0,1:T(8,128)} %copy-done.8) | copy-start | bytes 2457604
  73.7 163.8 %reduce-scatter.18.cloned.1.call-start = ((), (), s32[]{:S(2)}) async-start(), calls=%async_computation.14 | async-start | bytes 1310720
  126.6 113.1 %copy-start.6 = (bf16[128,5,3,64]{0,3,2,1:T(8,128)(2,1)}, bf16[128,5,3,64]{0,3,2,1:T(8,128)(2,1)S(1)}, u32[]{:S(2)}) copy-start(bf16[128,5,3,64]{0,3,2,1:T(8,128)(2,1)S(1)} %copy.131) | copy-start | bytes 737284
  191.3 48.3 %copy-start.19 = (f32[128]{0:T(128)}, f32[128]{0:T(128)S(1)}, u32[]{:S(2)}) copy-start(f32[128]{0:T(128)S(1)} %add_rsqrt_fusion) | copy-start | bytes 1540
  191.5 13.4 %copy-start.4 = (bf16[512,960]{0,1:T(8,128)(2,1)S(1)}, bf16[512,960]{0,1:T(8,128)(2,1)}, u32[]{:S(2)}) copy-start(bf16[512,960]{0,1:T(8,128)(2,1)} %all_gather.35) | copy-start | bytes 2949124
  201.5 3.4 copy-start.3
  207.3 0.8 copy-start.25
  207.3 1.0 copy-start.27
  213.0 113.0 %reduce-scatter.14.cloned.1.call-start = ((), (), s32[]{:S(2)}) async-start(), calls=%async_computation.8 | async-start | bytes 2785280 | tf_op jit(solution)/shard_map/reduce_scatter | solution.py:264
  239.5 4.5 copy-start.23
  261.6 0.9 copy-start.7
  261.6 94.5 %all-gather.14.cloned.1.call-start = ((), (), s32[]{:S(2)}) async-start(), calls=%async_computation.9 | async-start | bytes 2457600 | tf_op jit(solution)/shard_map/all_gather | solution.py:281
  263.4 176.3 %reduce-scatter.22.cloned.1.call-start = ((), (), s32[]{:S(2)}) async-start(), calls=%async_computation.16 | async-start | bytes 4147200
  263.4 2.4 copy-start.26
  263.4 2.4 copy-start.28
  269.5 1.0 copy-start.11
  326.0 3.0 copy-start.2
  328.8 0.9 copy-start.12
  329.3 1.3 copy-start.13
  330.6 20.9 %all-to-all-start = ((bf16[128,4,640]{0,2,1:T(8,128)(2,1)}), bf16[128,4,640]{0,2,1:T(8,128)(2,1)S(1)}, u32[]{:S(2)}, u32[]{:S(2)}) async-start(bf16[128,4,640]{0,2,1:T(8,128)(2,1)} %pad_maximum_fusion.6), calls=%async_computation.1 | async-start | bytes 1310720 | tf_op jit(solution)/shard_map/all_to_all | solution.py:291
  334.1 172.8 %reduce-scatter.20.cloned.1.call-start = ((), (), s32[]{:S(2)}) async-start(), calls=%async_computation.15 | async-start | bytes 1658880
  361.5 172.4 %reduce-scatter.16.cloned.1.call-start = ((), (), s32[]{:S(2)}) async-start(), calls=%async_computation.13 | async-start | bytes 1310720
  364.0 171.1 %copy-start.15 = (f32[960]{0:T(1024)S(1)}, f32[960]{0:T(1024)}, u32[]{:S(2)}) copy-start(f32[960]{0:T(1024)} %copy-done.14) | copy-start | bytes 11524
  364.0 171.1 %copy-start.17 = (f32[960]{0:T(1024)S(1)}, f32[960]{0:T(1024)}, u32[]{:S(2)}) copy-start(f32[960]{0:T(1024)} %copy-done.16) | copy-start | bytes 11524
  364.0 171.1 %copy-start.20 = (f32[128]{0:T(128)S(1)}, f32[128]{0:T(128)}, u32[]{:S(2)}) copy-start(f32[128]{0:T(128)} %copy-done.19) | copy-start | bytes 1540
  364.0 171.1 %copy-start.22 = (f32[128]{0:T(128)S(1)}, f32[128]{0:T(128)}, u32[]{:S(2)}) copy-start(f32[128]{0:T(128)} %copy-done.21) | copy-start | bytes 1540
  364.0 171.1 %copy-start.24 = (f32[128]{0:T(128)S(1)}, f32[128]{0:T(128)}, u32[]{:S(2)}) copy-start(f32[128]{0:T(128)} %copy-done.23) | copy-start | bytes 1540
  365.3 211.5 %all-gather.16.cloned.1.call-start = ((), (), s32[]{:S(2)}) async-start(), calls=%async_computation.10 | async-start | bytes 2304000 | tf_op jit(solution)/shard_map/all_gather | solution.py:317
  439.7 181.7 %all-gather.20.cloned.1.call-start = ((), (), s32[]{:S(2)}) async-start(), calls=%async_computation.12 | async-start | bytes 2820096 | tf_op jit(solution)/shard_map/all_gather | solution.py:321
Sparse Core Ops, SparseCore 0:
  15.2 48.1 all-gather.9
  71.0 44.2 all-gather.17
  116.8 71.9 all-gather.11
  213.1 24.2 reduce-scatter.17
  261.7 64.1 reduce-scatter.13
  328.0 28.0 all-gather.13
  359.8 79.8 reduce-scatter.21
  443.7 63.1 reduce-scatter.19
  510.0 23.8 reduce-scatter.15
  535.3 41.4 all-gather.15
  579.5 41.8 all-gather.19

commit v2 on v1

--- a/solution.py
+++ b/solution.py
@@ -136,6 +136,35 @@
             flops=20 * HD * cost, bytes_accessed=4 * all_kv.size, transcendentals=cost
         ),
     )(key_places, own_lanes, q_pad, d_att_pad, all_kv, totals, delta)
+
+
+def ring(axis):
+    size = lax.axis_size(axis)
+    return size, lax.axis_index(axis), [(i, (i + 1) % size) for i in range(size)]
+
+
+def ring_gather(block, axis):
+    size, me, hops = ring(axis)
+    held = [block]
+    for _ in range(size - 1):
+        held.append(lax.ppermute(held[-1], axis, hops))
+    ordered = [lax.select_n(lax.rem(me - j + size, size), *held) for j in range(size)]
+    return held[-1], jnp.concatenate(ordered, axis=0)
+
+
+def ring_reduce(values, axis):
+    size, me, hops = ring(axis)
+    count = values.shape[0] // size
+
+    def block(step):
+        which = lax.rem(me - 1 - step + 2 * size, size)
+        return lax.dynamic_slice_in_dim(values, which * count, count, 0)
+
+    total = block(0)
+    for step in range(1, size):
+        moved = lax.ppermute(total, axis, hops)
+        total = (moved.astype(jnp.float32) + block(step).astype(jnp.float32)).astype(jnp.bfloat16)
+    return total
 
 
 def per_device(
@@ -164,23 +193,22 @@
     key_places = sequence_places[:, None]
     own_lanes = jnp.tile(own_places, groups)[None, :]
 
-    first_pack = lax.all_gather(
+    last_block, first_pack = ring_gather(
         jnp.concatenate(
             [query_weight, key_weight, value_weight, attn_gain[:, None], mlp_gain[:, None]], axis=1
         ),
         "fsdp",
-        axis=0,
-        tiled=True,
     )
     qkv_full = first_pack[:, :qkv_cols]
     gain_one = first_pack[:, qkv_cols].astype(jnp.float32)
     gain_two = first_pack[:, qkv_cols + 1].astype(jnp.float32)
-    second_pack = lax.all_gather(
-        jnp.concatenate([gate_weight, up_weight, down_weight, out_weight], axis=1),
-        "fsdp",
-        axis=0,
-        tiled=True,
-    )
+    second_block, _ = lax.optimization_barrier(
+        (
+            jnp.concatenate([gate_weight, up_weight, down_weight, out_weight], axis=1),
+            last_block,
+        )
+    )
+    _, second_pack = ring_gather(second_block, "fsdp")
     gate_up_full = second_pack[:, : 2 * hidden]
     down_full = second_pack[:, 2 * hidden : 3 * hidden]
     out_full = second_pack[:, 3 * hidden :]
@@ -312,11 +340,11 @@
     ).astype(jnp.bfloat16)
 
     mlp_share = lax.psum_scatter(
-        mlp_grads, ("fsdp", "context"), scatter_dimension=0, tiled=True
+        ring_reduce(mlp_grads, "fsdp"), "context", scatter_dimension=0, tiled=True
     )
     mlp_owned = lax.all_gather(mlp_share, "context", axis=0, tiled=True).astype(jnp.float32)
     attn_share = lax.psum_scatter(
-        attn_grads, ("fsdp", "context"), scatter_dimension=0, tiled=True
+        ring_reduce(attn_grads, "fsdp"), "context", scatter_dimension=0, tiled=True
     )
     pieces = lax.all_gather(attn_share, ("context", "tensor"), axis=0)
     pieces = pieces.reshape(

time: 649 us -> 515 us (0.79)
  waiting for transfers between devices: 482 us -> 330 us
  other arithmetic: 17.4 us -> 27.3 us
  starting transfers between devices: 4.17 us -> 12.9 us
    ppermute x0 -> x4, waiting for transfers between devices: none -> 133 us  [the longest x2 77.2 us: ring_gather(): held.append(lax.ppermute(held[-1], axis, hops))]
    all_gather x2 -> x0, waiting for transfers between devices: 110 us -> none  [the longest x1 62.2 us: per_device(): lax.all_gather(jnp.concatenate([gate_weight, up_weight, down_weight, out_...]
    unnamed x15 -> x13, waiting for transfers between devices: 191 us -> 90.8 us
    reduce_scatter x1, waiting for transfers between devices: 54.9 us -> 7.58 us  [per_device(): lax.psum_scatter(dkv_terms, ('context', 'tensor'), scatter_dimension=0)]
    all_gather x1, waiting for transfers between devices: 26.2 us -> 0.01 us  [per_device(): all_kv = lax.all_gather(own_kv, ('context', 'tensor'), axis=0)]
    ppermute x0 -> x4, starting transfers between devices: none -> 7.9 us  [the longest x2 4.84 us: ring_gather(): held.append(lax.ppermute(held[-1], axis, hops))]
    unnamed x68 -> x90, local copies, waits for them, and re-layouts: 16.5 us -> 19 us
  transfers between devices with their start and end apart: 12 -> 14, of which waited for: 12 -> 13; matrix products, arithmetic and copies ran while one was open for 6% -> 10% of each run, Pallas kernels for 2% -> 0%
where the time goes in v2:
time: 515 us; the launch traced here: 514 us
  waiting for transfers between devices  330 us (64%)
  local copies, waits for them, and re-layouts  56.1 us (11%)
  other arithmetic  27.3 us (5%)
  matrix products  25.9 us (5%)
  Pallas kernels  25.1 us (5%)
  blocking collectives  21.7 us (4%)
  between operations  14.6 us (3%)
  starting transfers between devices  12.9 us (3%)
    unnamed x13, waiting for transfers between devices  90.8 us
    ppermute x2, waiting for transfers between devices, ring_gather(): held.append(lax.ppermute(held[-1], axis, hops))  77.2 us
    ppermute x2, waiting for transfers between devices, ring_reduce(): moved = lax.ppermute(total, axis, hops)  56.2 us
    all_gather x1, waiting for transfers between devices, per_device(): pieces = lax.all_gather(attn_share, ('context', 'tensor'), axis=0)  41.2 us
    all_gather x1, waiting for transfers between devices, per_device(): lax.all_gather(mlp_share, 'context', axis=0, tiled=True).astype(jnp.float32)  40.7 us
    unnamed x90, local copies, waits for them, and re-layouts  19 us
    pallas_call x1, Pallas kernels, attend_backward(): pl.pallas_call(backward_kernel, grid=(KV_HEADS,), in_specs=[places, own,...  14.9 us
    all_to_all x1, waiting for transfers between devices, per_device(): lax.all_to_all(quarters, 'tensor', split_axis=1, concat_axis=0, tiled=True)  14.2 us
  transfers between devices with their start and end apart: 14, of which 13 were waited for; matrix products, arithmetic and copies ran while one was open for 10% of the time, Pallas kernels for 0%

profile of v2, /device:TPU:0, one launch (start us, length us, event | category | flops | bytes accessed | tf_op | source)
XLA Modules:
  0.0 513.8 jit_solution(15198995425339955350)
XLA Ops:
  11.3 2.5 concatenate.57
  13.8 3.0 collective-permute-start
  17.5 34.4 %collective-permute-done = bf16[480,1602]{1,0:T(8,128)(2,1)} collective-permute-done((bf16[480,1602]{1,0:T(8,128)(2,1)S(1)}, bf16[480,1602]{1,0:T(8,128)(2,1)}, u32[]{:S(2)}, u32[]{:S(2)}) %collective-permute-start) | collective-permute-done | bytes 1537952 | tf_op jit(solution)/shard_map/ppermute | solution.py:150
  51.9 1.7 broadcast_select_fusion.3
  58.2 1.9 pad_maximum_fusion
  60.1 1.8 collective-permute-start.1
  64.0 11.9 %all_gather.27 = bf16[512,960]{0,1:T(8,128)(2,1)} all-gather(bf16[128,960]{0,1:T(8,128)(2,1)S(1)} %copy-done.14), channel_id=1, replica_groups=mesh['fsdp'=2,'context'=4,'tensor'=4] {'tensor'}, dimensions={0}, use_global_device_ids=true | all-gather | bytes 1228800 | tf_op jit(solution)/shard_map/all_gather | solution.py:240
  79.9 42.8 %collective-permute-done.1 = bf16[480,2880]{1,0:T(8,128)(2,1)} collective-permute-done((bf16[480,2880]{1,0:T(8,128)(2,1)S(1)}, bf16[480,2880]{1,0:T(8,128)(2,1)}, u32[]{:S(2)}, u32[]{:S(2)}) %collective-permute-start.1) | collective-permute-done | bytes 2764832 | tf_op jit(solution)/shard_map/ppermute | solution.py:150
  122.7 3.2 broadcast_select_fusion
  127.7 1.6 fusion.1
  129.3 10.3 %shard_map.203 = (bf16[5,64,384]{2,1,0:T(8,128)(2,1)}, f32[5,1,384]{2,1,0:T(1,128)}) custom-call(s32[2048,1]{1,0:T(8,128)} %copy.130.key_places_ref, s32[1,384]{1,0:T(1,128)} %bitcast.127, bf16[5,384,128]{2,1,0:T(8,128)(2,1)} %pad.8.q_ref, bf16[16,5,128,128]{3,2,1,0:T(8,128)(2,1)} %bitcast.129), custom_call_target="tpu_custom_call" | custom-call | flops 2013265920 | bytes 2621440 | tf_op jit(solution)/shard_map/pallas_call | solution.py:108
  141.4 2.6 multiply_reduce_fusion
  144.2 9.9 %all_gather.26 = bf16[512,960]{0,1:T(8,128)(2,1)S(1)} all-gather(bf16[128,960]{0,1:T(8,128)(2,1)S(1)} %multiply_convert_fusion.3), channel_id=1, replica_groups=mesh['fsdp'=2,'context'=4,'tensor'=4] {'tensor'}, dimensions={0}, use_global_device_ids=true | all-gather | bytes 1228800 | tf_op jit(solution)/shard_map/all_gather | solution.py:239
  154.0 1.6 fusion.47
  155.9 2.4 multiply_convert_fusion.1
  159.4 2.4 convolution_convert_fusion.2
  161.8 2.3 copy.151
  164.2 25.2 %reduce-scatter.18.cloned.1.call-done = bf16[128,960]{1,0:T(8,128)(2,1)} async-done(((bf16[512,960]{1,0:T(8,128)(2,1)}), bf16[128,960]{1,0:T(8,128)(2,1)}) %reduce-scatter.18.cloned.1.call-update) | async-done | bytes 245776
  195.9 14.9 %shard_map.204 = (f32[5,64,384]{2,1,0:T(8,128)}, bf16[16,5,128,128]{3,2,1,0:T(8,128)(2,1)}) custom-call(s32[2048,1]{1,0:T(8,128)} %copy.130.key_places_ref, s32[1,384]{1,0:T(1,128)} %bitcast.128, bf16[5,384,128]{2,1,0:T(8,128)(2,1)} %pad.8.q_ref, bf16[5,384,128]{2,1,0:T(8,128)(2,1)} %pad.9.d_att_ref, bf16[16,5,128,128]{3,2,1,0:T(8,128)(2,1)} %bitcast.130, ...), custom_call_target="tpu_custom_call" | custom-call | flops 5033164800 | bytes 5242880 | tf_op jit(solution)/shard_map/pallas_call | solution.py:126
  212.5 3.0 convolution_convert_fusion
  215.8 2.3 fusion.4
  219.8 1.5 collective-permute-start.3
  221.3 40.6 %collective-permute-done.3 = bf16[480,1920]{1,0:T(8,128)(2,1)} collective-permute-done((bf16[480,1920]{1,0:T(8,128)(2,1)}, bf16[480,1920]{1,0:T(8,128)(2,1)}, u32[]{:S(2)}, u32[]{:S(2)}) %collective-permute-start.3) | collective-permute-done | bytes 1843232 | tf_op jit(solution)/shard_map/ppermute | solution.py:165
  261.9 3.3 add_convert_fusion
  267.5 7.6 %reduce-scatter.14.cloned.1.call-done = bf16[1,5,128,128]{3,2,1,0:T(8,128)(2,1)} async-done(((bf16[16,5,128,128]{3,2,1,0:T(8,128)(2,1)}), bf16[1,5,128,128]{3,2,1,0:T(8,128)(2,1)}) %reduce-scatter.14.cloned.1.call-update) | async-done | bytes 163856 | tf_op jit(solution)/shard_map/reduce_scatter | solution.py:292
  277.8 2.1 pad_maximum_fusion.6
  279.9 4.2 all-to-all-start
  284.3 3.2 fusion.23
  287.5 14.2 %all-to-all-done = bf16[128,4,640]{0,2,1:T(8,128)(2,1)} async-done(((bf16[128,4,640]{0,2,1:T(8,128)(2,1)}), bf16[128,4,640]{0,2,1:T(8,128)(2,1)}, u32[]{:S(2)}, u32[]{:S(2)}) %all-to-all-start) | async-done | bytes 655392 | tf_op jit(solution)/shard_map/all_to_all | solution.py:319
  303.1 2.1 all-gather.8.cloned.1.call-done
  305.2 1.9 convolution_convert_fusion.5
  308.4 1.5 collective-permute-start.2
  309.9 15.6 %collective-permute-done.2 = bf16[480,642]{0,1:T(8,128)(2,1)S(1)} collective-permute-done((bf16[480,642]{0,1:T(8,128)(2,1)S(1)}, bf16[480,642]{0,1:T(8,128)(2,1)S(1)}, u32[]{:S(2)}, u32[]{:S(2)}) %collective-permute-start.2) | collective-permute-done | bytes 616352 | tf_op jit(solution)/shard_map/ppermute | solution.py:165
  327.1 3.0 convolution_convert_fusion.3
  330.1 2.3 copy.149
  332.5 15.2 %reduce-scatter.22.cloned.1.call-done = bf16[120,1920]{1,0:T(8,128)(2,1)} async-done(((bf16[480,1920]{1,0:T(8,128)(2,1)}), bf16[120,1920]{1,0:T(8,128)(2,1)}) %reduce-scatter.22.cloned.1.call-update) | async-done | bytes 460816
  348.0 24.9 %reduce-scatter.20.cloned.1.call-done = bf16[120,642]{1,0:T(8,128)(2,1)} async-done(((bf16[480,642]{1,0:T(8,128)(2,1)}), bf16[120,642]{1,0:T(8,128)(2,1)}) %reduce-scatter.20.cloned.1.call-update) | async-done | bytes 154096
  373.0 1.7 copy.154
  374.7 25.3 %reduce-scatter.16.cloned.1.call-done = bf16[128,960]{1,0:T(8,128)(2,1)} async-done(((bf16[512,960]{1,0:T(8,128)(2,1)}), bf16[128,960]{1,0:T(8,128)(2,1)}) %reduce-scatter.16.cloned.1.call-update) | async-done | bytes 245776
  402.5 40.7 %all-gather.10.cloned.1.call-done = bf16[480,1920]{1,0:T(8,128)(2,1)} async-done(((bf16[120,1920]{1,0:T(8,128)(2,1)}), bf16[480,1920]{1,0:T(8,128)(2,1)}) %all-gather.10.cloned.1.call-update) | async-done | bytes 1843216 | tf_op jit(solution)/shard_map/all_gather | solution.py:345
  443.1 3.4 fusion.51
  446.5 41.2 %all-gather.14.cloned.1.call-done = bf16[16,120,642]{1,2,0:T(8,128)(2,1)} async-done(((bf16[1,120,642]{1,2,0:T(8,128)(2,1)}), bf16[16,120,642]{1,2,0:T(8,128)(2,1)}) %all-gather.14.cloned.1.call-update) | async-done | bytes 2465296 | tf_op jit(solution)/shard_map/all_gather | solution.py:349
  487.7 2.1 bitcast_convert_fusion
  489.9 2.2 slice_bitcast_fusion
  493.7 2.0 copy.144
  495.7 2.6 reshape.171
  502.6 2.0 copy.147
  504.6 2.6 reshape.174
  (179 shorter events, 48.4 us)
Async XLA Ops:
  7.2 122.1 %all-gather.12.cloned.1.call-start = ((), (), s32[]{:S(2)}) async-start(), calls=%async_computation.9 | async-start | bytes 2785280 | tf_op jit(solution)/shard_map/all_gather | solution.py:227
  9.7 7.2 %copy-start.32 = (s32[1,2048]{1,0:T(1,128)S(1)}, s32[1,2048]{1,0:T(1,128)}, u32[]{:S(2)}) copy-start(s32[1,2048]{1,0:T(1,128)} %param.13) | copy-start | bytes 24580
  11.3 6.0 %copy-start.8 = (bf16[128,960]{0,1:T(8,128)(2,1)S(1)}, bf16[128,960]{0,1:T(8,128)(2,1)}, u32[]{:S(2)}) copy-start(bf16[128,960]{0,1:T(8,128)(2,1)} %param.12) | copy-start | bytes 737284
  13.8 38.1 %collective-permute-start = (bf16[480,1602]{1,0:T(8,128)(2,1)S(1)}, bf16[480,1602]{1,0:T(8,128)(2,1)}, u32[]{:S(2)}, u32[]{:S(2)}) collective-permute-start(bf16[480,1602]{1,0:T(8,128)(2,1)S(1)} %concatenate.57), channel_id=1, source_target_pairs={{0,16},{16,0},{1,17},{17,1},{2,18},{18,2},{3,19},{19,3},{4,20},{20... | collective-permute-start | bytes 4613768 | tf_op jit(solution)/shard_map/ppermute | solution.py:150
  17.3 44.6 %copy-start.21 = (f32[128,64]{1,0:T(8,128)}, f32[128,64]{1,0:T(8,128)S(1)}, u32[]{:S(2)}) copy-start(f32[128,64]{1,0:T(8,128)S(1)} %get-tuple-element.63) | copy-start | bytes 98308
  17.5 36.5 %copy-start.33 = (f32[128]{0:T(128)}, f32[128]{0:T(128)S(1)}, u32[]{:S(2)}) copy-start(f32[128]{0:T(128)S(1)} %add_rsqrt_fusion.1) | copy-start | bytes 1540
  53.6 2.1 copy-start.4
  53.6 2.1 copy-start.6
  54.2 1.5 copy-start.25
  58.1 5.9 %copy-start.14 = (bf16[128,960]{0,1:T(8,128)(2,1)S(1)}, bf16[128,960]{0,1:T(8,128)(2,1)}, u32[]{:S(2)}) copy-start(bf16[128,960]{0,1:T(8,128)(2,1)} %param.14) | copy-start | bytes 737284
  58.1 131.3 %reduce-scatter.18.cloned.1.call-start = ((), (), s32[]{:S(2)}) async-start(), calls=%async_computation.12 | async-start | bytes 1310720
  60.1 16.9 %copy-start.3 = (bf16[480,2880]{1,0:T(8,128)(2,1)}, bf16[480,2880]{1,0:T(8,128)(2,1)S(1)}, u32[]{:S(2)}) copy-start(bf16[480,2880]{1,0:T(8,128)(2,1)S(1)} %pad_maximum_fusion) | copy-start | bytes 8294404
  60.1 62.6 %collective-permute-start.1 = (bf16[480,2880]{1,0:T(8,128)(2,1)S(1)}, bf16[480,2880]{1,0:T(8,128)(2,1)}, u32[]{:S(2)}, u32[]{:S(2)}) collective-permute-start(bf16[480,2880]{1,0:T(8,128)(2,1)S(1)} %pad_maximum_fusion), channel_id=1, source_target_pairs={{0,16},{16,0},{1,17},{17,1},{2,18},{18,2},{3,19},{19,3},{4,20},{20... | collective-permute-start | bytes 8294408 | tf_op jit(solution)/shard_map/ppermute | solution.py:150
  62.0 15.0 %copy-start.30 = (f32[128,64]{0,1:T(8,128)}, f32[128,64]{0,1:T(8,128)S(1)}, u32[]{:S(2)}) copy-start(f32[128,64]{0,1:T(8,128)S(1)} %copy.124) | copy-start | bytes 98308
  125.8 1.9 copy-start
  141.4 12.7 %copy-start.1 = (bf16[480,2880]{1,0:T(8,128)(2,1)S(1)}, bf16[480,2880]{1,0:T(8,128)(2,1)}, u32[]{:S(2)}) copy-start(bf16[480,2880]{1,0:T(8,128)(2,1)} %copy-done) | copy-start | bytes 8294404
  154.0 1.6 copy-start.24
  154.0 1.6 copy-start.19
  154.0 1.9 copy-start.23
  158.3 1.0 copy-start.39
  161.8 29.6 %copy-start.15 = (bf16[128,960]{0,1:T(8,128)(2,1)S(1)}, bf16[128,960]{0,1:T(8,128)(2,1)}, u32[]{:S(2)}) copy-start(bf16[128,960]{0,1:T(8,128)(2,1)} %param.14) | copy-start | bytes 737284
  164.1 27.5 %copy-start.2 = (bf16[960,960]{1,0:T(8,128)(2,1)S(1)}, bf16[960,960]{1,0:T(8,128)(2,1)}, u32[]{:S(2)}) copy-start(bf16[960,960]{1,0:T(8,128)(2,1)} %fusion.1) | copy-start | bytes 5529604
  164.1 27.6 %copy-start.13 = (bf16[128,5,3,64]{0,3,2,1:T(8,128)(2,1)S(1)}, bf16[128,5,3,64]{0,3,2,1:T(8,128)(2,1)}, u32[]{:S(2)}) copy-start(bf16[128,5,3,64]{0,3,2,1:T(8,128)(2,1)} %copy-done.12) | copy-start | bytes 737284
  164.1 111.0 %reduce-scatter.14.cloned.1.call-start = ((), (), s32[]{:S(2)}) async-start(), calls=%async_computation.6 | async-start | bytes 2785280 | tf_op jit(solution)/shard_map/reduce_scatter | solution.py:292
  190.5 2.5 copy-start.10
  191.6 1.4 copy-start.17
  210.8 94.5 %all-gather.8.cloned.1.call-start = ((), (), s32[]{:S(2)}) async-start(), calls=%async_computation.7 | async-start | bytes 2457600 | tf_op jit(solution)/shard_map/all_gather | solution.py:309
  215.6 132.2 %reduce-scatter.22.cloned.1.call-start = ((), (), s32[]{:S(2)}) async-start(), calls=%async_computation.14 | async-start | bytes 2304000
  218.2 1.6 copy-start.7
  219.8 42.1 %collective-permute-start.3 = (bf16[480,1920]{1,0:T(8,128)(2,1)}, bf16[480,1920]{1,0:T(8,128)(2,1)}, u32[]{:S(2)}, u32[]{:S(2)}) collective-permute-start(bf16[480,1920]{1,0:T(8,128)(2,1)} %fusion.3), channel_id=1, source_target_pairs={{0,16},{16,0},{1,17},{17,1},{2,18},{18,2},{3,19},{19,3},{4,20},{20... | collective-permute-start | bytes 5529608 | tf_op jit(solution)/shard_map/ppermute | solution.py:165
  265.2 1.3 copy-start.31
  266.6 9.7 %copy-start.22 = (f32[128,64]{1,0:T(8,128)S(1)}, f32[128,64]{1,0:T(8,128)}, u32[]{:S(2)}) copy-start(f32[128,64]{1,0:T(8,128)} %copy-done.21) | copy-start | bytes 98308
  275.1 2.4 copy-start.18
  277.8 6.5 %copy-start.5 = (bf16[480,1602]{1,0:T(8,128)(2,1)S(1)}, bf16[480,1602]{1,0:T(8,128)(2,1)}, u32[]{:S(2)}) copy-start(bf16[480,1602]{1,0:T(8,128)(2,1)} %copy-done.4) | copy-start | bytes 4613764
  277.8 6.5 %copy-start.9 = (bf16[128,960]{0,1:T(8,128)(2,1)S(1)}, bf16[128,960]{0,1:T(8,128)(2,1)}, u32[]{:S(2)}) copy-start(bf16[128,960]{0,1:T(8,128)(2,1)} %param.12) | copy-start | bytes 737284
  277.8 6.5 %copy-start.34 = (f32[128]{0:T(128)S(1)}, f32[128]{0:T(128)}, u32[]{:S(2)}) copy-start(f32[128]{0:T(128)} %copy-done.33) | copy-start | bytes 1540
  279.9 21.9 %all-to-all-start = ((bf16[128,4,640]{0,2,1:T(8,128)(2,1)}), bf16[128,4,640]{0,2,1:T(8,128)(2,1)}, u32[]{:S(2)}, u32[]{:S(2)}) async-start(bf16[128,4,640]{0,2,1:T(8,128)(2,1)} %pad_maximum_fusion.6), calls=%async_computation.1 | async-start | bytes 1310720 | tf_op jit(solution)/shard_map/all_to_all | solution.py:319
  284.1 88.9 %reduce-scatter.20.cloned.1.call-start = ((), (), s32[]{:S(2)}) async-start(), calls=%async_computation.13 | async-start | bytes 921600
  305.2 1.9 copy-start.37
  308.4 18.7 %copy-start.20 = (bf16[960,640]{1,0:T(8,128)(2,1)S(1)}, bf16[960,640]{1,0:T(8,128)(2,1)}, u32[]{:S(2)}) copy-start(bf16[960,640]{1,0:T(8,128)(2,1)} %pad_maximum_fusion.3) | copy-start | bytes 3686404
  308.4 17.1 %collective-permute-start.2 = (bf16[480,642]{0,1:T(8,128)(2,1)S(1)}, bf16[480,642]{0,1:T(8,128)(2,1)S(1)}, u32[]{:S(2)}, u32[]{:S(2)}) collective-permute-start(bf16[480,642]{0,1:T(8,128)(2,1)S(1)} %constant_dynamic-slice_fusion), channel_id=1, source_target_pairs={{0,16},{16,0},{1,17},{17,1},{2,18},{18,2},{3,19},{19,3},{4,20},{20... | collective-permute-start | bytes 1848968 | tf_op jit(solution)/shard_map/ppermute | solution.py:165
  327.0 73.0 %reduce-scatter.16.cloned.1.call-start = ((), (), s32[]{:S(2)}) async-start(), calls=%async_computation.11 | async-start | bytes 1310720
  330.1 71.1 %copy-start.11 = (bf16[128,960]{0,1:T(8,128)(2,1)S(1)}, bf16[128,960]{0,1:T(8,128)(2,1)}, u32[]{:S(2)}) copy-start(bf16[128,960]{0,1:T(8,128)(2,1)} %copy-done.10) | copy-start | bytes 737284
  330.1 71.1 %copy-start.16 = (bf16[128,960]{0,1:T(8,128)(2,1)S(1)}, bf16[128,960]{0,1:T(8,128)(2,1)}, u32[]{:S(2)}) copy-start(bf16[128,960]{0,1:T(8,128)(2,1)} %param.14) | copy-start | bytes 737284
  330.1 71.1 %copy-start.28 = (f32[128,960]{0,1:T(8,128)S(1)}, f32[128,960]{0,1:T(8,128)}, u32[]{:S(2)}) copy-start(f32[128,960]{0,1:T(8,128)} %get-tuple-element.61) | copy-start | bytes 1474564
  330.1 71.2 %copy-start.36 = (f32[128]{0:T(128)S(1)}, f32[128]{0:T(128)}, u32[]{:S(2)}) copy-start(f32[128]{0:T(128)} %copy-done.35) | copy-start | bytes 1540
  332.5 110.7 %all-gather.10.cloned.1.call-start = ((), (), s32[]{:S(2)}) async-start(), calls=%async_computation.8 | async-start | bytes 2304000 | tf_op jit(solution)/shard_map/all_gather | solution.py:345
  347.7 140.0 %all-gather.14.cloned.1.call-start = ((), (), s32[]{:S(2)}) async-start(), calls=%async_computation.10 | async-start | bytes 2820096 | tf_op jit(solution)/shard_map/all_gather | solution.py:349
  (6 other events, 5.0 us)
Sparse Core Ops, SparseCore 0:
  58.2 45.5 all-gather.11
  164.2 25.0 reduce-scatter.17
  210.9 64.1 reduce-scatter.13
  277.1 28.0 all-gather.7
  308.0 39.6 reduce-scatter.21
  350.4 22.5 reduce-scatter.19
  376.1 23.9 reduce-scatter.15
  401.6 41.4 all-gather.9
  445.9 41.8 all-gather.13

commit v3 on v2

--- a/solution.py
+++ b/solution.py
@@ -246,21 +246,17 @@
     d_gate = (d_act * up * sig * (1.0 + gate * (1.0 - sig))).astype(jnp.bfloat16)
     d_up = (d_act * gate * sig).astype(jnp.bfloat16)
     d_gate_up = jnp.concatenate([d_gate, d_up], axis=1)
-    d_normed_two = lax.psum_scatter(
+    d_normed_two = ring_reduce(
         lax.dot_general(
             d_gate_up, gate_up_full, COLS_MATCH, preferred_element_type=jnp.float32
         ).astype(jnp.bfloat16),
         "tensor",
-        scatter_dimension=0,
-        tiled=True,
     ).astype(jnp.float32)
-    feed = lax.psum_scatter(
+    feed = ring_reduce(
         lax.dot_general(act, down_full, COLS_MATCH, preferred_element_type=jnp.float32).astype(
             jnp.bfloat16
         ),
         "tensor",
-        scatter_dimension=0,
-        tiled=True,
     )
     output = (residual + feed.astype(jnp.float32)).astype(jnp.bfloat16)
     mlp_grads = jnp.concatenate(

time: 515 us -> 477 us (0.926)
  waiting for transfers between devices: 330 us -> 296 us
  local copies, waits for them, and re-layouts: 56.1 us -> 50 us
    unnamed x13 -> x9, waiting for transfers between devices: 90.8 us -> 46 us
    ppermute x2 -> x8, waiting for transfers between devices: 56.2 us -> 85.8 us  [ring_reduce(): moved = lax.ppermute(total, axis, hops)]
    all_gather x1, waiting for transfers between devices: 40.7 us -> 19.4 us  [per_device(): lax.all_gather(mlp_share, 'context', axis=0, tiled=True).astype(jnp.float32)]
    unnamed x90 -> x86, local copies, waits for them, and re-layouts: 19 us -> 11.2 us
  transfers between devices with their start and end apart: 14 -> 18, of which waited for: 13 -> 17; matrix products, arithmetic and copies ran while one was open for 10% -> 11% of each run, Pallas kernels for 0% -> 0%
where the time goes in v3:
time: 477 us; the launch traced here: 476 us
  waiting for transfers between devices  296 us (62%)
  local copies, waits for them, and re-layouts  50 us (10%)
  other arithmetic  31.2 us (7%)
  Pallas kernels  25.2 us (5%)
  matrix products  22.7 us (5%)
  blocking collectives  21.7 us (5%)
  between operations  15 us (3%)
  starting transfers between devices  13.5 us (3%)
    ppermute x8, waiting for transfers between devices, ring_reduce(): moved = lax.ppermute(total, axis, hops)  85.8 us
    ppermute x2, waiting for transfers between devices, ring_gather(): held.append(lax.ppermute(held[-1], axis, hops))  77.2 us
    unnamed x9, waiting for transfers between devices  46 us
    all_gather x1, waiting for transfers between devices, per_device(): pieces = lax.all_gather(attn_share, ('context', 'tensor'), axis=0)  41.2 us
    all_gather x1, waiting for transfers between devices, per_device(): lax.all_gather(mlp_share, 'context', axis=0, tiled=True).astype(jnp.float32)  19.4 us
    all_to_all x1, waiting for transfers between devices, per_device(): lax.all_to_all(quarters, 'tensor', split_axis=1, concat_axis=0, tiled=True)  14.9 us
    pallas_call x1, Pallas kernels, attend_backward(): pl.pallas_call(backward_kernel, grid=(KV_HEADS,), in_specs=[places, own,...  14.9 us
    all_gather x1, blocking collectives, per_device(): cot_rows = lax.all_gather(cotangent, 'tensor', axis=0, tiled=True)  11.9 us
  transfers between devices with their start and end apart: 18, of which 17 were waited for; matrix products, arithmetic and copies ran while one was open for 11% of the time, Pallas kernels for 0%

profile of v3, /device:TPU:0, one launch (start us, length us, event | category | flops | bytes accessed | tf_op | source)
XLA Modules:
  0.0 475.5 jit_solution(303856818052631167)
XLA Ops:
  11.3 2.5 concatenate.57
  13.8 3.0 collective-permute-start
  17.5 34.4 %collective-permute-done = bf16[480,1602]{1,0:T(8,128)(2,1)} collective-permute-done((bf16[480,1602]{1,0:T(8,128)(2,1)S(1)}, bf16[480,1602]{1,0:T(8,128)(2,1)}, u32[]{:S(2)}, u32[]{:S(2)}) %collective-permute-start) | collective-permute-done | bytes 1537952 | tf_op jit(solution)/shard_map/ppermute | solution.py:150
  51.9 1.7 broadcast_select_fusion.3
  58.2 1.9 pad_maximum_fusion
  60.1 1.8 collective-permute-start.1
  64.0 11.9 %all_gather.27 = bf16[512,960]{0,1:T(8,128)(2,1)} all-gather(bf16[128,960]{0,1:T(8,128)(2,1)S(1)} %copy-done.13), channel_id=1, replica_groups=mesh['fsdp'=2,'context'=4,'tensor'=4] {'tensor'}, dimensions={0}, use_global_device_ids=true | all-gather | bytes 1228800 | tf_op jit(solution)/shard_map/all_gather | solution.py:240
  79.9 42.8 %collective-permute-done.1 = bf16[480,2880]{1,0:T(8,128)(2,1)} collective-permute-done((bf16[480,2880]{1,0:T(8,128)(2,1)S(1)}, bf16[480,2880]{1,0:T(8,128)(2,1)}, u32[]{:S(2)}, u32[]{:S(2)}) %collective-permute-start.1) | collective-permute-done | bytes 2764832 | tf_op jit(solution)/shard_map/ppermute | solution.py:150
  122.7 3.2 broadcast_select_fusion
  127.8 1.6 fusion.1
  129.3 10.3 %shard_map.203 = (bf16[5,64,384]{2,1,0:T(8,128)(2,1)}, f32[5,1,384]{2,1,0:T(1,128)}) custom-call(s32[2048,1]{1,0:T(8,128)} %copy.130.key_places_ref, s32[1,384]{1,0:T(1,128)} %bitcast.125, bf16[5,384,128]{2,1,0:T(8,128)(2,1)} %pad.8.q_ref, bf16[16,5,128,128]{3,2,1,0:T(8,128)(2,1)} %bitcast.127), custom_call_target="tpu_custom_call" | custom-call | flops 2013265920 | bytes 2621440 | tf_op jit(solution)/shard_map/pallas_call | solution.py:108
  141.4 2.6 multiply_reduce_fusion
  144.2 9.8 %all_gather.26 = bf16[512,960]{0,1:T(8,128)(2,1)S(1)} all-gather(bf16[128,960]{0,1:T(8,128)(2,1)S(1)} %multiply_convert_fusion.3), channel_id=1, replica_groups=mesh['fsdp'=2,'context'=4,'tensor'=4] {'tensor'}, dimensions={0}, use_global_device_ids=true | all-gather | bytes 1228800 | tf_op jit(solution)/shard_map/all_gather | solution.py:239
  154.0 1.6 fusion.47
  156.0 2.4 multiply_convert_fusion.1
  161.2 5.3 %collective-permute-done.5 = bf16[128,960]{0,1:T(8,128)(2,1)S(1)} collective-permute-done((bf16[128,960]{0,1:T(8,128)(2,1)S(1)}, bf16[128,960]{0,1:T(8,128)(2,1)S(1)}, u32[]{:S(2)}, u32[]{:S(2)}) %collective-permute-start.5) | collective-permute-done | bytes 245792 | tf_op jit(solution)/shard_map/ppermute | solution.py:165
  167.6 5.7 %collective-permute-done.6 = bf16[128,960]{0,1:T(8,128)(2,1)} collective-permute-done((bf16[128,960]{0,1:T(8,128)(2,1)S(1)}, bf16[128,960]{0,1:T(8,128)(2,1)}, u32[]{:S(2)}, u32[]{:S(2)}) %collective-permute-start.6) | collective-permute-done | bytes 245792 | tf_op jit(solution)/shard_map/ppermute | solution.py:165
  174.5 5.6 %collective-permute-done.7 = bf16[128,960]{0,1:T(8,128)(2,1)S(1)} collective-permute-done((bf16[128,960]{0,1:T(8,128)(2,1)S(1)}, bf16[128,960]{0,1:T(8,128)(2,1)S(1)}, u32[]{:S(2)}, u32[]{:S(2)}) %collective-permute-start.7) | collective-permute-done | bytes 245792 | tf_op jit(solution)/shard_map/ppermute | solution.py:165
  184.9 14.9 %shard_map.204 = (f32[5,64,384]{2,1,0:T(8,128)}, bf16[16,5,128,128]{3,2,1,0:T(8,128)(2,1)}) custom-call(s32[2048,1]{1,0:T(8,128)} %copy.130.key_places_ref, s32[1,384]{1,0:T(1,128)} %bitcast.126, bf16[5,384,128]{2,1,0:T(8,128)(2,1)} %pad.8.q_ref, bf16[5,384,128]{2,1,0:T(8,128)(2,1)} %pad.9.d_att_ref, bf16[16,5,128,128]{3,2,1,0:T(8,128)(2,1)} %bitcast.128, ...), custom_call_target="tpu_custom_call" | custom-call | flops 5033164800 | bytes 5242880 | tf_op jit(solution)/shard_map/pallas_call | solution.py:126
  201.5 3.0 convolution_convert_fusion
  204.8 2.4 fusion.4
  212.6 36.9 %collective-permute-done.9 = bf16[480,1920]{1,0:T(8,128)(2,1)} collective-permute-done((bf16[480,1920]{1,0:T(8,128)(2,1)}, bf16[480,1920]{1,0:T(8,128)(2,1)}, u32[]{:S(2)}, u32[]{:S(2)}) %collective-permute-start.9) | collective-permute-done | bytes 1843232 | tf_op jit(solution)/shard_map/ppermute | solution.py:165
  249.4 3.3 add_convert_fusion
  254.5 9.9 %reduce-scatter.8.cloned.1.call-done = bf16[1,5,128,128]{3,2,1,0:T(8,128)(2,1)} async-done(((bf16[16,5,128,128]{3,2,1,0:T(8,128)(2,1)}), bf16[1,5,128,128]{3,2,1,0:T(8,128)(2,1)}) %reduce-scatter.8.cloned.1.call-update) | async-done | bytes 163856 | tf_op jit(solution)/shard_map/reduce_scatter | solution.py:288
  267.8 2.1 pad_maximum_fusion.6
  269.9 4.2 all-to-all-start
  274.3 2.6 fusion.23
  276.9 14.9 %all-to-all-done = bf16[128,4,640]{0,2,1:T(8,128)(2,1)} async-done(((bf16[128,4,640]{0,2,1:T(8,128)(2,1)}), bf16[128,4,640]{0,2,1:T(8,128)(2,1)}, u32[]{:S(2)}, u32[]{:S(2)}) %all-to-all-start) | async-done | bytes 655392 | tf_op jit(solution)/shard_map/all_to_all | solution.py:315
  293.2 1.5 all-gather.8.cloned.1.call-done
  294.7 1.9 convolution_convert_fusion.5
  297.9 1.5 collective-permute-start.8
  299.4 15.6 %collective-permute-done.8 = bf16[480,642]{0,1:T(8,128)(2,1)S(1)} collective-permute-done((bf16[480,642]{0,1:T(8,128)(2,1)S(1)}, bf16[480,642]{0,1:T(8,128)(2,1)S(1)}, u32[]{:S(2)}, u32[]{:S(2)}) %collective-permute-start.8) | collective-permute-done | bytes 616352 | tf_op jit(solution)/shard_map/ppermute | solution.py:165
  316.6 20.6 %reduce-scatter.12.cloned.1.call-done = bf16[120,1920]{1,0:T(8,128)(2,1)} async-done(((bf16[480,1920]{1,0:T(8,128)(2,1)}), bf16[120,1920]{1,0:T(8,128)(2,1)}) %reduce-scatter.12.cloned.1.call-update) | async-done | bytes 460816
  337.3 25.2 %reduce-scatter.10.cloned.1.call-done = bf16[120,642]{1,0:T(8,128)(2,1)} async-done(((bf16[480,642]{1,0:T(8,128)(2,1)}), bf16[120,642]{1,0:T(8,128)(2,1)}) %reduce-scatter.10.cloned.1.call-update) | async-done | bytes 154096
  362.5 1.7 copy.150
  364.3 2.0 convolution_convert_fusion.3
  366.5 5.6 %collective-permute-done.2 = bf16[128,960]{0,1:T(8,128)(2,1)S(1)} collective-permute-done((bf16[128,960]{0,1:T(8,128)(2,1)S(1)}, bf16[128,960]{0,1:T(8,128)(2,1)S(1)}, u32[]{:S(2)}, u32[]{:S(2)}) %collective-permute-start.2) | collective-permute-done | bytes 245792 | tf_op jit(solution)/shard_map/ppermute | solution.py:165
  372.2 5.6 %collective-permute-done.3 = bf16[128,960]{0,1:T(8,128)(2,1)S(1)} collective-permute-done((bf16[128,960]{0,1:T(8,128)(2,1)S(1)}, bf16[128,960]{0,1:T(8,128)(2,1)S(1)}, u32[]{:S(2)}, u32[]{:S(2)}) %collective-permute-start.3) | collective-permute-done | bytes 245792 | tf_op jit(solution)/shard_map/ppermute | solution.py:165
  378.2 5.6 %collective-permute-done.4 = bf16[128,960]{0,1:T(8,128)(2,1)S(1)} collective-permute-done((bf16[128,960]{0,1:T(8,128)(2,1)S(1)}, bf16[128,960]{0,1:T(8,128)(2,1)S(1)}, u32[]{:S(2)}, u32[]{:S(2)}) %collective-permute-start.4) | collective-permute-done | bytes 245792 | tf_op jit(solution)/shard_map/ppermute | solution.py:165
  385.1 19.4 %all-gather.10.cloned.1.call-done = bf16[480,1920]{1,0:T(8,128)(2,1)} async-done(((bf16[120,1920]{1,0:T(8,128)(2,1)}), bf16[480,1920]{1,0:T(8,128)(2,1)}) %all-gather.10.cloned.1.call-update) | async-done | bytes 1843216 | tf_op jit(solution)/shard_map/all_gather | solution.py:341
  404.6 3.4 fusion.51
  407.9 41.2 %all-gather.14.cloned.1.call-done = bf16[16,120,642]{1,2,0:T(8,128)(2,1)} async-done(((bf16[1,120,642]{1,2,0:T(8,128)(2,1)}), bf16[16,120,642]{1,2,0:T(8,128)(2,1)}) %all-gather.14.cloned.1.call-update) | async-done | bytes 2465296 | tf_op jit(solution)/shard_map/all_gather | solution.py:345
  449.1 2.1 bitcast_convert_fusion
  451.3 2.2 slice_bitcast_fusion
  455.1 2.0 copy.144
  457.1 2.6 reshape.171
  464.0 2.0 copy.147
  466.0 2.6 reshape.174
  (187 shorter events, 53.7 us)
Async XLA Ops:
  7.2 122.1 %all-gather.12.cloned.1.call-start = ((), (), s32[]{:S(2)}) async-start(), calls=%async_computation.7 | async-start | bytes 2785280 | tf_op jit(solution)/shard_map/all_gather | solution.py:227
  9.7 7.2 %copy-start.32 = (s32[1,2048]{1,0:T(1,128)S(1)}, s32[1,2048]{1,0:T(1,128)}, u32[]{:S(2)}) copy-start(s32[1,2048]{1,0:T(1,128)} %param.13) | copy-start | bytes 24580
  11.3 6.0 %copy-start.10 = (bf16[128,960]{0,1:T(8,128)(2,1)S(1)}, bf16[128,960]{0,1:T(8,128)(2,1)}, u32[]{:S(2)}) copy-start(bf16[128,960]{0,1:T(8,128)(2,1)} %param.12) | copy-start | bytes 737284
  13.8 38.1 %collective-permute-start = (bf16[480,1602]{1,0:T(8,128)(2,1)S(1)}, bf16[480,1602]{1,0:T(8,128)(2,1)}, u32[]{:S(2)}, u32[]{:S(2)}) collective-permute-start(bf16[480,1602]{1,0:T(8,128)(2,1)S(1)} %concatenate.57), channel_id=1, source_target_pairs={{0,16},{16,0},{1,17},{17,1},{2,18},{18,2},{3,19},{19,3},{4,20},{20... | collective-permute-start | bytes 4613768 | tf_op jit(solution)/shard_map/ppermute | solution.py:150
  17.3 44.6 %copy-start.21 = (f32[128,64]{1,0:T(8,128)}, f32[128,64]{1,0:T(8,128)S(1)}, u32[]{:S(2)}) copy-start(f32[128,64]{1,0:T(8,128)S(1)} %get-tuple-element.64) | copy-start | bytes 98308
  17.5 36.5 %copy-start.33 = (f32[128]{0:T(128)}, f32[128]{0:T(128)S(1)}, u32[]{:S(2)}) copy-start(f32[128]{0:T(128)S(1)} %add_rsqrt_fusion.1) | copy-start | bytes 1540
  53.6 2.1 copy-start.4
  53.6 2.1 copy-start.6
  58.1 5.9 %copy-start.13 = (bf16[128,960]{0,1:T(8,128)(2,1)S(1)}, bf16[128,960]{0,1:T(8,128)(2,1)}, u32[]{:S(2)}) copy-start(bf16[128,960]{0,1:T(8,128)(2,1)} %param.14) | copy-start | bytes 737284
  58.1 206.3 %reduce-scatter.8.cloned.1.call-start = ((), (), s32[]{:S(2)}) async-start(), calls=%async_computation.4 | async-start | bytes 2785280 | tf_op jit(solution)/shard_map/reduce_scatter | solution.py:288
  60.1 16.9 %copy-start.3 = (bf16[480,2880]{1,0:T(8,128)(2,1)}, bf16[480,2880]{1,0:T(8,128)(2,1)S(1)}, u32[]{:S(2)}) copy-start(bf16[480,2880]{1,0:T(8,128)(2,1)S(1)} %pad_maximum_fusion) | copy-start | bytes 8294404
  60.1 62.6 %collective-permute-start.1 = (bf16[480,2880]{1,0:T(8,128)(2,1)S(1)}, bf16[480,2880]{1,0:T(8,128)(2,1)}, u32[]{:S(2)}, u32[]{:S(2)}) collective-permute-start(bf16[480,2880]{1,0:T(8,128)(2,1)S(1)} %pad_maximum_fusion), channel_id=1, source_target_pairs={{0,16},{16,0},{1,17},{17,1},{2,18},{18,2},{3,19},{19,3},{4,20},{20... | collective-permute-start | bytes 8294408 | tf_op jit(solution)/shard_map/ppermute | solution.py:150
  62.0 15.0 %copy-start.31 = (f32[128,64]{0,1:T(8,128)}, f32[128,64]{0,1:T(8,128)S(1)}, u32[]{:S(2)}) copy-start(f32[128,64]{0,1:T(8,128)S(1)} %copy.124) | copy-start | bytes 98308
  125.8 1.9 copy-start
  141.4 12.7 %copy-start.1 = (bf16[480,2880]{1,0:T(8,128)(2,1)S(1)}, bf16[480,2880]{1,0:T(8,128)(2,1)}, u32[]{:S(2)}) copy-start(bf16[480,2880]{1,0:T(8,128)(2,1)} %copy-done) | copy-start | bytes 8294404
  154.0 1.6 copy-start.24
  154.0 1.6 copy-start.19
  154.0 1.9 copy-start.23
  160.8 21.2 %copy-start.14 = (bf16[128,960]{0,1:T(8,128)(2,1)S(1)}, bf16[128,960]{0,1:T(8,128)(2,1)}, u32[]{:S(2)}) copy-start(bf16[128,960]{0,1:T(8,128)(2,1)} %param.14) | copy-start | bytes 737284
  160.8 5.7 %collective-permute-start.5 = (bf16[128,960]{0,1:T(8,128)(2,1)S(1)}, bf16[128,960]{0,1:T(8,128)(2,1)S(1)}, u32[]{:S(2)}, u32[]{:S(2)}) collective-permute-start(bf16[128,960]{0,1:T(8,128)(2,1)S(1)} %constant_dynamic-slice_fusion.1), channel_id=1, source_target_pairs={{0,1},{1,2},{2,3},{3,0},{4,5},{5,6},{6,7},{7,4},{8,9},{9,10},{10,1... | collective-permute-start | bytes 737288 | tf_op jit(solution)/shard_map/ppermute | solution.py:165
  161.2 21.0 %copy-start.2 = (bf16[960,960]{1,0:T(8,128)(2,1)S(1)}, bf16[960,960]{1,0:T(8,128)(2,1)}, u32[]{:S(2)}) copy-start(bf16[960,960]{1,0:T(8,128)(2,1)} %fusion.1) | copy-start | bytes 5529604
  161.2 21.0 %copy-start.9 = (bf16[128,5,3,64]{0,3,2,1:T(8,128)(2,1)S(1)}, bf16[128,5,3,64]{0,3,2,1:T(8,128)(2,1)}, u32[]{:S(2)}) copy-start(bf16[128,5,3,64]{0,3,2,1:T(8,128)(2,1)} %copy-done.8) | copy-start | bytes 737284
  167.5 5.8 %collective-permute-start.6 = (bf16[128,960]{0,1:T(8,128)(2,1)S(1)}, bf16[128,960]{0,1:T(8,128)(2,1)}, u32[]{:S(2)}, u32[]{:S(2)}) collective-permute-start(bf16[128,960]{0,1:T(8,128)(2,1)S(1)} %add_convert_fusion.5), channel_id=1, source_target_pairs={{0,1},{1,2},{2,3},{3,0},{4,5},{5,6},{6,7},{7,4},{8,9},{9,10},{10,1... | collective-permute-start | bytes 737288 | tf_op jit(solution)/shard_map/ppermute | solution.py:165
  174.4 5.7 %collective-permute-start.7 = (bf16[128,960]{0,1:T(8,128)(2,1)S(1)}, bf16[128,960]{0,1:T(8,128)(2,1)S(1)}, u32[]{:S(2)}, u32[]{:S(2)}) collective-permute-start(bf16[128,960]{0,1:T(8,128)(2,1)S(1)} %add_convert_fusion.4), channel_id=1, source_target_pairs={{0,1},{1,2},{2,3},{3,0},{4,5},{5,6},{6,7},{7,4},{8,9},{9,10},{10,1... | collective-permute-start | bytes 737288 | tf_op jit(solution)/shard_map/ppermute | solution.py:165
  199.8 94.9 %all-gather.8.cloned.1.call-start = ((), (), s32[]{:S(2)}) async-start(), calls=%async_computation.5 | async-start | bytes 2457600 | tf_op jit(solution)/shard_map/all_gather | solution.py:305
  204.6 132.6 %reduce-scatter.12.cloned.1.call-start = ((), (), s32[]{:S(2)}) async-start(), calls=%async_computation.10 | async-start | bytes 2304000
  207.2 1.6 copy-start.7
  207.2 3.1 copy-start.29
  208.9 40.5 %collective-permute-start.9 = (bf16[480,1920]{1,0:T(8,128)(2,1)}, bf16[480,1920]{1,0:T(8,128)(2,1)}, u32[]{:S(2)}, u32[]{:S(2)}) collective-permute-start(bf16[480,1920]{1,0:T(8,128)(2,1)} %fusion.3), channel_id=1, source_target_pairs={{0,16},{16,0},{1,17},{17,1},{2,18},{18,2},{3,19},{19,3},{4,20},{20... | collective-permute-start | bytes 5529608 | tf_op jit(solution)/shard_map/ppermute | solution.py:165
  253.6 12.7 %copy-start.22 = (f32[128,64]{1,0:T(8,128)S(1)}, f32[128,64]{1,0:T(8,128)}, u32[]{:S(2)}) copy-start(f32[128,64]{1,0:T(8,128)} %copy-done.21) | copy-start | bytes 98308
  264.4 3.0 copy-start.18
  267.7 6.5 %copy-start.30 = (bf16[128,5,64]{0,2,1:T(8,128)(2,1)}, bf16[128,5,64]{0,2,1:T(8,128)(2,1)S(1)}, u32[]{:S(2)}) copy-start(bf16[128,5,64]{0,2,1:T(8,128)(2,1)S(1)} %copy.137) | copy-start | bytes 245764
  267.7 6.5 %copy-start.5 = (bf16[480,1602]{1,0:T(8,128)(2,1)S(1)}, bf16[480,1602]{1,0:T(8,128)(2,1)}, u32[]{:S(2)}) copy-start(bf16[480,1602]{1,0:T(8,128)(2,1)} %copy-done.4) | copy-start | bytes 4613764
  267.7 6.5 %copy-start.11 = (bf16[128,960]{0,1:T(8,128)(2,1)S(1)}, bf16[128,960]{0,1:T(8,128)(2,1)}, u32[]{:S(2)}) copy-start(bf16[128,960]{0,1:T(8,128)(2,1)} %param.12) | copy-start | bytes 737284
  267.8 6.5 %copy-start.34 = (f32[128]{0:T(128)S(1)}, f32[128]{0:T(128)}, u32[]{:S(2)}) copy-start(f32[128]{0:T(128)} %copy-done.33) | copy-start | bytes 1540
  269.9 21.9 %all-to-all-start = ((bf16[128,4,640]{0,2,1:T(8,128)(2,1)}), bf16[128,4,640]{0,2,1:T(8,128)(2,1)}, u32[]{:S(2)}, u32[]{:S(2)}) async-start(bf16[128,4,640]{0,2,1:T(8,128)(2,1)} %pad_maximum_fusion.6), calls=%async_computation.1 | async-start | bytes 1310720 | tf_op jit(solution)/shard_map/all_to_all | solution.py:315
  274.1 88.4 %reduce-scatter.10.cloned.1.call-start = ((), (), s32[]{:S(2)}) async-start(), calls=%async_computation.9 | async-start | bytes 921600
  294.7 1.9 copy-start.37
  297.9 17.1 %collective-permute-start.8 = (bf16[480,642]{0,1:T(8,128)(2,1)S(1)}, bf16[480,642]{0,1:T(8,128)(2,1)S(1)}, u32[]{:S(2)}, u32[]{:S(2)}) collective-permute-start(bf16[480,642]{0,1:T(8,128)(2,1)S(1)} %constant_dynamic-slice_fusion), channel_id=1, source_target_pairs={{0,16},{16,0},{1,17},{17,1},{2,18},{18,2},{3,19},{19,3},{4,20},{20... | collective-permute-start | bytes 1848968 | tf_op jit(solution)/shard_map/ppermute | solution.py:165
  315.4 48.9 %copy-start.20 = (bf16[960,640]{1,0:T(8,128)(2,1)S(1)}, bf16[960,640]{1,0:T(8,128)(2,1)}, u32[]{:S(2)}) copy-start(bf16[960,640]{1,0:T(8,128)(2,1)} %pad_maximum_fusion.3) | copy-start | bytes 3686404
  316.5 88.0 %all-gather.10.cloned.1.call-start = ((), (), s32[]{:S(2)}) async-start(), calls=%async_computation.6 | async-start | bytes 2304000 | tf_op jit(solution)/shard_map/all_gather | solution.py:341
  337.2 111.9 %all-gather.14.cloned.1.call-start = ((), (), s32[]{:S(2)}) async-start(), calls=%async_computation.8 | async-start | bytes 2820096 | tf_op jit(solution)/shard_map/all_gather | solution.py:345
  366.3 17.5 %copy-start.15 = (bf16[128,960]{0,1:T(8,128)(2,1)S(1)}, bf16[128,960]{0,1:T(8,128)(2,1)}, u32[]{:S(2)}) copy-start(bf16[128,960]{0,1:T(8,128)(2,1)} %param.14) | copy-start | bytes 737284
  366.3 17.5 %copy-start.17 = (bf16[128,960]{0,1:T(8,128)(2,1)S(1)}, bf16[128,960]{0,1:T(8,128)(2,1)}, u32[]{:S(2)}) copy-start(bf16[128,960]{0,1:T(8,128)(2,1)} %copy-done.16) | copy-start | bytes 737284
  366.3 17.5 %copy-start.36 = (f32[128]{0:T(128)S(1)}, f32[128]{0:T(128)}, u32[]{:S(2)}) copy-start(f32[128]{0:T(128)} %copy-done.35) | copy-start | bytes 1540
  366.4 5.7 %collective-permute-start.2 = (bf16[128,960]{0,1:T(8,128)(2,1)S(1)}, bf16[128,960]{0,1:T(8,128)(2,1)S(1)}, u32[]{:S(2)}, u32[]{:S(2)}) collective-permute-start(bf16[128,960]{0,1:T(8,128)(2,1)S(1)} %constant_dynamic-slice_fusion.2), channel_id=1, source_target_pairs={{0,1},{1,2},{2,3},{3,0},{4,5},{5,6},{6,7},{7,4},{8,9},{9,10},{10,1... | collective-permute-start | bytes 737288 | tf_op jit(solution)/shard_map/ppermute | solution.py:165
  372.2 5.7 %collective-permute-start.3 = (bf16[128,960]{0,1:T(8,128)(2,1)S(1)}, bf16[128,960]{0,1:T(8,128)(2,1)S(1)}, u32[]{:S(2)}, u32[]{:S(2)}) collective-permute-start(bf16[128,960]{0,1:T(8,128)(2,1)S(1)} %add_convert_fusion.9), channel_id=1, source_target_pairs={{0,1},{1,2},{2,3},{3,0},{4,5},{5,6},{6,7},{7,4},{8,9},{9,10},{10,1... | collective-permute-start | bytes 737288 | tf_op jit(solution)/shard_map/ppermute | solution.py:165
  377.9 5.9 %collective-permute-start.4 = (bf16[128,960]{0,1:T(8,128)(2,1)S(1)}, bf16[128,960]{0,1:T(8,128)(2,1)S(1)}, u32[]{:S(2)}, u32[]{:S(2)}) collective-permute-start(bf16[128,960]{0,1:T(8,128)(2,1)S(1)} %add_convert_fusion.8), channel_id=1, source_target_pairs={{0,1},{1,2},{2,3},{3,0},{4,5},{5,6},{6,7},{7,4},{8,9},{9,10},{10,1... | collective-permute-start | bytes 737288 | tf_op jit(solution)/shard_map/ppermute | solution.py:165
  (10 other events, 10.8 us)
Sparse Core Ops, SparseCore 0:
  58.2 45.5 all-gather.11
  199.9 64.4 reduce-scatter.7
  266.6 28.1 all-gather.7
  297.5 39.6 reduce-scatter.11
  339.9 22.5 reduce-scatter.9
  363.9 40.5 all-gather.9
  407.3 41.8 all-gather.13
